TPU v7x, 32 devices: a whole 2x2x4 slice. The times are simulated.
32 devices in a mesh: expert: 4 (over x, core), fsdp: 8 (over z, y).
Axes of the slice: x: 2, y: 2, z: 4, core: 2. Of those that a mesh axis runs over, the one named last changes fastest.
Arguments:
- inputs: bfloat16 [12288, 1024], P(('expert', 'fsdp')), may hold values from -6 to 6
- w_qkv: bfloat16 [1024, 3072], P(('expert', 'fsdp')), may hold values from -0.1875 to 0.1875
- w_out: bfloat16 [1024, 1024], P(('expert', 'fsdp')), may hold values from -3 to 3
- attn_gain: bfloat16 [1024], P(('expert', 'fsdp')), may hold values from 0.5 to 1.5
- moe_gain: bfloat16 [1024], P(('expert', 'fsdp')), may hold values from 0.5 to 1.5
- w_router: bfloat16 [1024, 4], P(('expert', 'fsdp')), may hold values from -0.125 to 0.125
- bias_table: bfloat16 [512], P(('expert', 'fsdp')), may hold values from -4 to 4
- w_gate: bfloat16 [4, 1024, 2816], P('expert', None, 'fsdp'), may hold values from -0.1875 to 0.1875
- w_up: bfloat16 [4, 1024, 2816], P('expert', None, 'fsdp'), may hold values from -0.1875 to 0.1875
- w_down: bfloat16 [4, 2816, 1024], P('expert', 'fsdp'), may hold values from -0.15625 to 0.15625
- routes: int32 [12288, 2], P(('expert', 'fsdp')), may hold values from 0 to 3, as said below
- slot_order: int32 [12288, 2], P(('expert', 'fsdp')), may hold values from 0 to 240, as said below
- group_map: int32 [32], P(('expert', 'fsdp')), may hold values from 0 to 1, as said below
- buckets: int32 [1152], replicated, may hold values from 0 to 31, as said below
- grad_output: bfloat16 [12288, 1024], P(('expert', 'fsdp')), may hold values from -6 to 6
Outputs:
- output: bfloat16 [12288, 1024], P(('expert', 'fsdp'))
- router_losses: float32 [32, 2], P(('expert', 'fsdp'))
- grad_inputs: float32 [12288, 1024], P(('expert', 'fsdp'))
- grad_w_qkv: float32 [1024, 3072], P(('expert', 'fsdp'))
- grad_w_out: float32 [1024, 1024], P(('expert', 'fsdp'))
- grad_attn_gain: float32 [1024], P(('expert', 'fsdp'))
- grad_moe_gain: float32 [1024], P(('expert', 'fsdp'))
- grad_w_router: float32 [1024, 4], P(('expert', 'fsdp'))
- grad_bias_table: float32 [512], P(('expert', 'fsdp'))
- grad_w_gate: float32 [4, 1024, 2816], P('expert', None, 'fsdp')
- grad_w_up: float32 [4, 1024, 2816], P('expert', None, 'fsdp')
- grad_w_down: float32 [4, 2816, 1024], P('expert', 'fsdp')
Inputs may be any that keep to these rules, and one draw needn't show every extreme that they name: `routes`: the two experts of a token differ. `slot_order`: within one routing group the choices that name one expert hold the distinct slots 0, 1, 2 and so on up to 239, and every further choice holds 240 and is dropped; in every draw one expert is named by more than 240 choices in every routing group. `group_map`: within a line each of its 2 prompts is named by exactly 4 continuations. `buckets`: non-decreasing in the distance, 0 at distance 0, every bucket used.
All inputs are finite; a program needn't handle non-finite values.
Results may differ from a plain program's by a relative error of at most 0.015.
Values may be sent and summed in bfloat16 or wider, within the bound.
A program may use at most 320 MiB of HBM per device.

v0:
```python
import functools

import jax
import jax.numpy as jnp
from jax import lax
from jax.experimental import pallas as pl
from jax.experimental.pallas import tpu as pltpu
from jax.sharding import PartitionSpec as P


D = 1024
HEADS = 16
HDIM = 64
BUCKETS = 32
TOPK = 2
PLEN = 1024
CLEN = 128
G_LINE = 2

EPSILON = 1e-06
ZLOSS_FACTOR = 0.001
BALANCE_FACTOR = 0.01
MASK_VALUE = -1e30
LOG2E = 1.4426950408889634
HIGHEST = lax.Precision.HIGHEST
TILE = 256
HALF = 128
SPAN_BLOCKS = (PLEN + CLEN) // HALF
BF = jnp.bfloat16
F32 = jnp.float32
NT = (((1,), (1,)), ((), ()))
TN = (((0,), (0,)), ((), ()))


def rms_scale(values, scale_row):
    inverse = lax.rsqrt(jnp.mean(values * values, axis=-1, keepdims=True) + EPSILON)
    return values * inverse * scale_row


def route_local(normed, router, routes):
    logits = jnp.dot(normed, router, precision=HIGHEST)
    log_total = jax.nn.logsumexp(logits, axis=-1)
    chances = jnp.exp(logits - log_total[:, None])
    expert_ids = jnp.arange(router.shape[1], dtype=jnp.int32)
    first_hot = (routes[:, 0:1] == expert_ids[None, :]).astype(F32)
    second_hot = (routes[:, 1:2] == expert_ids[None, :]).astype(F32)
    first_chance = jnp.sum(chances * first_hot, axis=-1)
    second_chance = jnp.sum(chances * second_hot, axis=-1)
    both_chances = first_chance + second_chance
    gate_pair = jnp.stack([first_chance / both_chances, second_chance / both_chances], -1)
    z_loss = jnp.mean(log_total * log_total)
    expert_share = jnp.sum(first_hot + second_hot, axis=0) / (TOPK * routes.shape[0])
    balance = router.shape[1] * jnp.sum(expert_share * jnp.mean(chances, axis=0))
    return (gate_pair, jnp.stack([z_loss, balance]))


class Shape:
    def __init__(self, fsdp_count):
        self.srcs = fsdp_count
        self.hp = HEADS // fsdp_count
        self.width = self.hp * HDIM
        self.part = PLEN // fsdp_count
        self.rows = G_LINE * self.part + CLEN
        self.spt = TILE // self.part
        self.tiles = PLEN // TILE
        self.pairs = fsdp_count // 2
        self.prompt_pairs = self.pairs // G_LINE
        self.units = G_LINE * self.tiles + self.pairs


def order_conts(sh, group_ref, perm_ref):
    counts = [jnp.int32(0), jnp.int32(sh.srcs // G_LINE)]
    for c in range(sh.srcs):
        first = group_ref[c] == 0
        perm_ref[jnp.where(first, counts[0], counts[1])] = jnp.int32(c)
        step = first.astype(jnp.int32)
        counts = [counts[0] + step, counts[1] + 1 - step]


def build_bias(sh, table_ref, bucket_ref, bias_ref):
    bucket = bucket_ref[...]
    for h in range(sh.hp):
        dist = jnp.zeros(bucket.shape, F32)
        for b in range(BUCKETS):
            dist = jnp.where(bucket == b, table_ref[h, b] * LOG2E, dist)
        bias_ref[h, 0] = jnp.full((HALF, HALF), MASK_VALUE, F32)
        before = jnp.full((1, HALF), MASK_VALUE, F32)
        for n in range(SPAN_BLOCKS):
            now = dist[n : n + 1, :]
            both = jnp.broadcast_to(jnp.concatenate([before, now], axis=1), (HALF, 2 * HALF))
            turned = pltpu.roll(both, HALF, 1, stride=1, stride_axis=0)
            bias_ref[h, 1 + n] = turned[:, :HALF]
            before = now


def head_mask(sh, h):
    if sh.hp == 1:
        return None
    lane = lax.broadcasted_iota(jnp.int32, (1, sh.width), 1)
    return (lane >= h * HDIM) & (lane < (h + 1) * HDIM)


def only_head(sh, h, x):
    mask = head_mask(sh, h)
    return x if mask is None else jnp.where(mask, x, jnp.zeros_like(x))


def prompt_rows_of(sh, ref, g, t, part):
    lanes = slice(part * sh.width, (part + 1) * sh.width)
    start = pl.multiple_of(g * sh.part, sh.part)
    return jnp.concatenate(
        [ref[t * sh.spt + s, pl.ds(start, sh.part), lanes] for s in range(sh.spt)], axis=0
    )


def cont_rows_of(sh, ref, c, part):
    lanes = slice(part * sh.width, (part + 1) * sh.width)
    return ref[c, G_LINE * sh.part :, lanes]


def put_prompt_rows(sh, ref, g, t, part, value):
    lanes = slice(part * sh.width, (part + 1) * sh.width)
    start = pl.multiple_of(g * sh.part, sh.part)
    for s in range(sh.spt):
        ref[t * sh.spt + s, pl.ds(start, sh.part), lanes] = value[
            s * sh.part : (s + 1) * sh.part
        ].astype(ref.dtype)


def transpose_low(x):
    return x.astype(F32).T.astype(BF)


def add_bias(scores, bias_ref, h, base, step_q):
    rows = []
    for a in range(2):
        cols = []
        for b in range(2):
            part = scores[a * HALF : (a + 1) * HALF, b * HALF : (b + 1) * HALF]
            cols.append(part * LOG2E + bias_ref[h, base + b * step_q - a])
        rows.append(jnp.concatenate(cols, axis=1))
    return jnp.concatenate(rows, axis=0)


def fold_max(x):
    return jnp.max(x.reshape(-1, 8, x.shape[-1]), axis=0)


def fold_sum(x):
    return jnp.sum(x.reshape(-1, 8, x.shape[-1]), axis=0)


def attn_forward_kernel(
    sh, group_ref, table_ref, bucket_ref, x_ref, o_ref, ot_ref, lse_ref, bias, vt, vtc, sc, perm
):
    order_conts(sh, group_ref, perm)
    build_bias(sh, table_ref, bucket_ref, bias)

    def make_vt(i, _):
        g, t = i // sh.tiles, lax.rem(i, sh.tiles)
        vt[i] = transpose_low(prompt_rows_of(sh, x_ref, g, t, 2))
        return 0

    lax.fori_loop(0, G_LINE * sh.tiles, make_vt, 0)

    def make_vtc(c, _):
        vtc[c] = transpose_low(cont_rows_of(sh, x_ref, c, 2))
        return 0

    lax.fori_loop(0, sh.srcs, make_vtc, 0)

    def scores_tile(keys, qh, base, step_q, kt, peaks):
        out = []
        for h in range(sh.hp):
            s = lax.dot_general(keys, qh[h], NT, preferred_element_type=F32)
            s = add_bias(s, bias, h, base, step_q)
            sc[h, pl.ds(pl.multiple_of(kt * TILE, TILE), TILE), :] = s
            out.append(jnp.maximum(peaks[h], fold_max(s)))
        return tuple(out)

    def value_tile(g, kt, peaks, carry):
        out = []
        for h in range(sh.hp):
            total, acc = carry[h]
            p = jnp.exp2(sc[h, pl.ds(pl.multiple_of(kt * TILE, TILE), TILE), :] - peaks[h])
            total = total + fold_sum(p)
            values = vt[g * sh.tiles + kt, h * HDIM : (h + 1) * HDIM, :]
            acc = acc + jnp.dot(values, p.astype(BF), preferred_element_type=F32)
            out.append((total, acc))
        return tuple(out)

    first_peaks = tuple(jnp.full((8, TILE), MASK_VALUE, F32) for _ in range(sh.hp))
    first_carry = tuple(
        (jnp.zeros((8, TILE), F32), jnp.zeros((HDIM, TILE), F32)) for _ in range(sh.hp)
    )

    def finish(unit, peaks, carry):
        outs = []
        for h in range(sh.hp):
            total = jnp.sum(carry[h][0], axis=0, keepdims=True)
            outs.append(carry[h][1] / total)
            lse_ref[unit, h : h + 1, :] = peaks[h] + jnp.log2(total)
        whole = jnp.concatenate(outs, axis=0) if sh.hp > 1 else outs[0]
        ot_ref[unit] = whole
        return whole.T

    def prompt_unit(i, _):
        g, qt = i // sh.tiles, lax.rem(i, sh.tiles)
        q = prompt_rows_of(sh, x_ref, g, qt, 0) * BF(HDIM**-0.5)
        qh = [only_head(sh, h, q) for h in range(sh.hp)]

        def first(kt, peaks):
            keys = prompt_rows_of(sh, x_ref, g, kt, 1)
            return scores_tile(keys, qh, 2 * (qt - kt) + 1, 1, kt, peaks)

        peaks = lax.fori_loop(0, qt + 1, first, first_peaks)
        peaks = [jnp.max(p, axis=0, keepdims=True) for p in peaks]
        carry = lax.fori_loop(0, qt + 1, lambda kt, c: value_tile(g, kt, peaks, c), first_carry)
        put_prompt_rows(sh, o_ref, g, qt, 0, finish(i, peaks, carry))
        return 0

    lax.fori_loop(0, G_LINE * sh.tiles, prompt_unit, 0)

    def cont_unit(i, _):
        conts = [perm[2 * i], perm[2 * i + 1]]
        g = i // sh.prompt_pairs
        q = jnp.concatenate([cont_rows_of(sh, x_ref, c, 0) for c in conts], axis=0)
        q = q * BF(HDIM**-0.5)
        qh = [only_head(sh, h, q) for h in range(sh.hp)]

        def first(kt, peaks):
            keys = prompt_rows_of(sh, x_ref, g, kt, 1)
            return scores_tile(keys, qh, SPAN_BLOCKS - 2 * kt, 0, kt, peaks)

        peaks = lax.fori_loop(0, sh.tiles, first, first_peaks)
        own = []
        next_peaks = []
        for h in range(sh.hp):
            parts = []
            for b in range(2):
                keys = cont_rows_of(sh, x_ref, conts[b], 1)
                s = lax.dot_general(
                    keys, qh[h][b * HALF : (b + 1) * HALF], NT, preferred_element_type=F32
                )
                parts.append(s * LOG2E + bias[h, 1])
            own.append(jnp.concatenate(parts, axis=1))
            next_peaks.append(jnp.maximum(peaks[h], fold_max(own[h])))
        peaks = [jnp.max(p, axis=0, keepdims=True) for p in next_peaks]
        start = []
        for h in range(sh.hp):
            p = jnp.exp2(own[h] - peaks[h])
            low = p.astype(BF)
            acc = jnp.concatenate(
                [
                    jnp.dot(
                        vtc[conts[b], h * HDIM : (h + 1) * HDIM, :],
                        low[:, b * HALF : (b + 1) * HALF],
                        preferred_element_type=F32,
                    )
                    for b in range(2)
                ],
                axis=1,
            )
            start.append((fold_sum(p), acc))
        carry = lax.fori_loop(
            0, sh.tiles, lambda kt, c: value_tile(g, kt, peaks, c), tuple(start)
        )
        done = finish(G_LINE * sh.tiles + i, peaks, carry)
        for b in range(2):
            o_ref[conts[b], G_LINE * sh.part :, :] = done[b * HALF : (b + 1) * HALF].astype(BF)
        return 0

    lax.fori_loop(0, sh.pairs, cont_unit, 0)


def attn_backward_kernel(
    sh,
    group_ref,
    table_ref,
    bucket_ref,
    x_ref,
    do_ref,
    ot_ref,
    lse_ref,
    dx_ref,
    dtable_ref,
    bias,
    dbias,
    ktr,
    ktc,
    dk,
    dv,
    perm,
):
    order_conts(sh, group_ref, perm)
    build_bias(sh, table_ref, bucket_ref, bias)
    dbias[...] = jnp.zeros_like(dbias)
    dk[...] = jnp.zeros_like(dk)
    dv[...] = jnp.zeros_like(dv)

    def make_kt(i, _):
        g, t = i // sh.tiles, lax.rem(i, sh.tiles)
        ktr[i] = transpose_low(prompt_rows_of(sh, x_ref, g, t, 1))
        return 0

    lax.fori_loop(0, G_LINE * sh.tiles, make_kt, 0)

    def make_ktc(c, _):
        ktc[c] = transpose_low(cont_rows_of(sh, x_ref, c, 1))
        return 0

    lax.fori_loop(0, sh.srcs, make_ktc, 0)

    def inner_terms(unit, do):
        outs = []
        turned = do.astype(F32).T
        for h in range(sh.hp):
            rows = slice(h * HDIM, (h + 1) * HDIM)
            prod = ot_ref[unit, rows, :] * turned[rows, :]
            outs.append(jnp.sum(prod, axis=0, keepdims=True))
        return outs

    def grads_tile(g, kt, qh, doh, lse, inner, base, step_q, dqs):
        keys = prompt_rows_of(sh, x_ref, g, kt, 1)
        values = prompt_rows_of(sh, x_ref, g, kt, 2)
        slot = g * sh.tiles + kt
        out = []
        dkey = dvalue = None
        for h in range(sh.hp):
            s = lax.dot_general(keys, qh[h], NT, preferred_element_type=F32)
            dp = lax.dot_general(values, doh[h], NT, preferred_element_type=F32)
            p = jnp.exp2(add_bias(s, bias, h, base, step_q) - lse[h])
            ds = p * (dp - inner[h])
            for a in range(2):
                for b in range(2):
                    dbias[h, base + b * step_q - a] += ds[
                        a * HALF : (a + 1) * HALF, b * HALF : (b + 1) * HALF
                    ]
            low = ds.astype(BF)
            more_k = jnp.dot(low, qh[h], preferred_element_type=F32)
            more_v = jnp.dot(p.astype(BF), doh[h], preferred_element_type=F32)
            dkey = more_k if dkey is None else dkey + more_k
            dvalue = more_v if dvalue is None else dvalue + more_v
            turned = ktr[slot, h * HDIM : (h + 1) * HDIM, :]
            out.append(dqs[h] + jnp.dot(turned, low, preferred_element_type=F32))
        dk[slot] += dkey
        dv[slot] += dvalue
        return tuple(out)

    def finish(dqs):
        whole = jnp.concatenate(dqs, axis=0) if sh.hp > 1 else dqs[0]
        return whole.T * (HDIM**-0.5)

    first_dq = tuple(jnp.zeros((HDIM, TILE), F32) for _ in range(sh.hp))

    def prompt_unit(i, _):
        g, qt = i // sh.tiles, lax.rem(i, sh.tiles)
        q = prompt_rows_of(sh, x_ref, g, qt, 0) * BF(HDIM**-0.5)
        do = prompt_rows_of(sh, do_ref, g, qt, 0)
        qh = [only_head(sh, h, q) for h in range(sh.hp)]
        doh = [only_head(sh, h, do) for h in range(sh.hp)]
        inner = inner_terms(i, do)
        lse = [lse_ref[i, h : h + 1, :] for h in range(sh.hp)]

        def body(kt, dqs):
            return grads_tile(g, kt, qh, doh, lse, inner, 2 * (qt - kt) + 1, 1, dqs)

        dqs = lax.fori_loop(0, qt + 1, body, first_dq)
        put_prompt_rows(sh, dx_ref, g, qt, 0, finish(dqs))
        return 0

    lax.fori_loop(0, G_LINE * sh.tiles, prompt_unit, 0)

    def cont_unit(i, _):
        conts = [perm[2 * i], perm[2 * i + 1]]
        unit = G_LINE * sh.tiles + i
        g = i // sh.prompt_pairs
        q = jnp.concatenate([cont_rows_of(sh, x_ref, c, 0) for c in conts], axis=0)
        q = q * BF(HDIM**-0.5)
        do = jnp.concatenate([cont_rows_of(sh, do_ref, c, 0) for c in conts], axis=0)
        qh = [only_head(sh, h, q) for h in range(sh.hp)]
        doh = [only_head(sh, h, do) for h in range(sh.hp)]
        inner = inner_terms(unit, do)
        lse = [lse_ref[unit, h : h + 1, :] for h in range(sh.hp)]

        def body(kt, dqs):
            return grads_tile(g, kt, qh, doh, lse, inner, SPAN_BLOCKS - 2 * kt, 0, dqs)

        dqs = lax.fori_loop(0, sh.tiles, body, first_dq)
        more = [[None] * 2 for _ in range(sh.hp)]
        for b in range(2):
            cols = slice(b * HALF, (b + 1) * HALF)
            keys = cont_rows_of(sh, x_ref, conts[b], 1)
            values = cont_rows_of(sh, x_ref, conts[b], 2)
            dkey = dvalue = None
            for h in range(sh.hp):
                s = lax.dot_general(keys, qh[h][cols], NT, preferred_element_type=F32)
                dp = lax.dot_general(values, doh[h][cols], NT, preferred_element_type=F32)
                p = jnp.exp2(s * LOG2E + bias[h, 1] - lse[h][:, cols])
                ds = p * (dp - inner[h][:, cols])
                dbias[h, 1] += ds
                low = ds.astype(BF)
                more_k = jnp.dot(low, qh[h][cols], preferred_element_type=F32)
                more_v = jnp.dot(p.astype(BF), doh[h][cols], preferred_element_type=F32)
                dkey = more_k if dkey is None else dkey + more_k
                dvalue = more_v if dvalue is None else dvalue + more_v
                turned = ktc[conts[b], h * HDIM : (h + 1) * HDIM, :]
                more[h][b] = jnp.dot(turned, low, preferred_element_type=F32)
            w = sh.width
            dx_ref[conts[b], G_LINE * sh.part :, w : 2 * w] = dkey.astype(BF)
            dx_ref[conts[b], G_LINE * sh.part :, 2 * w :] = dvalue.astype(BF)
        dqs = [dqs[h] + jnp.concatenate(more[h], axis=1) for h in range(sh.hp)]
        done = finish(dqs)
        for b in range(2):
            dx_ref[conts[b], G_LINE * sh.part :, : sh.width] = done[
                b * HALF : (b + 1) * HALF
            ].astype(BF)
        return 0

    lax.fori_loop(0, sh.pairs, cont_unit, 0)

    def put_keys(i, _):
        g, t = i // sh.tiles, lax.rem(i, sh.tiles)
        put_prompt_rows(sh, dx_ref, g, t, 1, dk[i])
        put_prompt_rows(sh, dx_ref, g, t, 2, dv[i])
        return 0

    lax.fori_loop(0, G_LINE * sh.tiles, put_keys, 0)

    bucket = bucket_ref[...]
    key_row = lax.broadcasted_iota(jnp.int32, (HALF, 2 * HALF), 0)
    for h in range(sh.hp):
        spread = []
        for n in range(SPAN_BLOCKS):
            wide = jnp.concatenate(
                [jnp.zeros((HALF, HALF), F32), dbias[h, 1 + n]], axis=1
            )
            for bit in range(7):
                moved = pltpu.roll(wide, 2 * HALF - (1 << bit), 1)
                wide = jnp.where((key_row & (1 << bit)) != 0, moved, wide)
            spread.append(jnp.sum(wide, axis=0, keepdims=True))
        rows = []
        for n in range(SPAN_BLOCKS):
            row = spread[n][:, HALF:]
            if n + 1 < SPAN_BLOCKS:
                row = row + spread[n + 1][:, :HALF]
            rows.append(row)
        by_dist = jnp.concatenate(rows, axis=0)
        sums = [
            jnp.sum(jnp.where(bucket == b, by_dist, 0.0), axis=0, keepdims=True)
            for b in range(BUCKETS)
        ]
        lanes = jnp.concatenate(sums, axis=0)
        dtable_ref[h * BUCKETS : (h + 1) * BUCKETS, :] = jnp.broadcast_to(
            jnp.sum(lanes, axis=1, keepdims=True), (BUCKETS, HALF)
        )


SMEM_SPEC = pl.BlockSpec(memory_space=pltpu.SMEM)
VMEM_SPEC = pl.BlockSpec(memory_space=pltpu.VMEM)
GRANT = 48 * 1024 * 1024


def attend_forward(sh, group, table, bucket, x):
    return pl.pallas_call(
        functools.partial(attn_forward_kernel, sh),
        out_shape=(
            jax.ShapeDtypeStruct((sh.srcs, sh.rows, sh.width), BF),
            jax.ShapeDtypeStruct((sh.units, sh.width, TILE), F32),
            jax.ShapeDtypeStruct((sh.units, 8, TILE), F32),
        ),
        in_specs=[SMEM_SPEC, SMEM_SPEC, VMEM_SPEC, VMEM_SPEC],
        out_specs=(VMEM_SPEC, VMEM_SPEC, VMEM_SPEC),
        scratch_shapes=[
            pltpu.VMEM((sh.hp, SPAN_BLOCKS + 1, HALF, HALF), F32),
            pltpu.VMEM((G_LINE * sh.tiles, sh.width, TILE), BF),
            pltpu.VMEM((sh.srcs, sh.width, HALF), BF),
            pltpu.VMEM((sh.hp, PLEN, TILE), F32),
            pltpu.SMEM((sh.srcs,), jnp.int32),
        ],
        compiler_params=pltpu.CompilerParams(vmem_limit_bytes=GRANT),
        cost_estimate=pl.CostEstimate(
            flops=10**10, bytes_accessed=8 * 10**6, transcendentals=5 * 10**6
        ),
        name="attend_forward",
    )(group, table, bucket, x)


def attend_backward(sh, group, table, bucket, x, do, ot, lse):
    return pl.pallas_call(
        functools.partial(attn_backward_kernel, sh),
        out_shape=(
            jax.ShapeDtypeStruct((sh.srcs, sh.rows, 3 * sh.width), BF),
            jax.ShapeDtypeStruct((sh.hp * BUCKETS, HALF), F32),
        ),
        in_specs=[SMEM_SPEC, SMEM_SPEC, VMEM_SPEC, VMEM_SPEC, VMEM_SPEC, VMEM_SPEC, VMEM_SPEC],
        out_specs=(VMEM_SPEC, VMEM_SPEC),
        scratch_shapes=[
            pltpu.VMEM((sh.hp, SPAN_BLOCKS + 1, HALF, HALF), F32),
            pltpu.VMEM((sh.hp, SPAN_BLOCKS + 1, HALF, HALF), F32),
            pltpu.VMEM((G_LINE * sh.tiles, sh.width, TILE), BF),
            pltpu.VMEM((sh.srcs, sh.width, HALF), BF),
            pltpu.VMEM((G_LINE * sh.tiles, TILE, sh.width), F32),
            pltpu.VMEM((G_LINE * sh.tiles, TILE, sh.width), F32),
            pltpu.SMEM((sh.srcs,), jnp.int32),
        ],
        compiler_params=pltpu.CompilerParams(vmem_limit_bytes=GRANT),
        cost_estimate=pl.CostEstimate(
            flops=2 * 10**10, bytes_accessed=12 * 10**6, transcendentals=5 * 10**6
        ),
        name="attend_backward",
    )(group, table, bucket, x, do, ot, lse)


def ring_order(count):
    deep, wide = 4, count // 4
    order = [a * wide for a in range(deep)]
    for turn, a in enumerate(reversed(range(deep))):
        row = [a * wide + b for b in range(1, wide)]
        order += row if turn % 2 == 0 else row[::-1]
    return order


def ring_hop(x, count, step):
    ring = ring_order(count)
    return lax.ppermute(x, "fsdp", [(ring[i], ring[(i + step) % count]) for i in range(count)])


def tied(*values):
    return lax.optimization_barrier(values)


class RingGather:
    def __init__(self, own, count):
        self.count = count
        self.chunks = [None] * count
        self.chunks[0] = own
        self.right = self.left = own
        self.done = 0
        self.steps = count // 2

    def step(self):
        self.done += 1
        s = self.done
        if s < self.steps:
            self.right = ring_hop(self.right, self.count, 1)
            self.left = ring_hop(self.left, self.count, -1)
        else:
            half = self.right.shape[0] // 2
            self.right = ring_hop(self.right[:half], self.count, 1)
            self.left = ring_hop(self.left[half:], self.count, -1)
        self.keep()

    def keep(self):
        s = self.done
        if s < self.steps:
            self.chunks[self.count - s] = self.right
            self.chunks[s] = self.left
        else:
            self.chunks[s] = (self.right, self.left)

    def tie(self, value):
        value, self.right, self.left = tied(value, self.right, self.left)
        self.keep()
        return value


class RingScatter:
    def __init__(self, part, count):
        self.part, self.count = part, count
        self.right = self.left = None
        self.done = 0
        self.steps = count // 2

    def step(self, after=None):
        count, s = self.count, self.done
        away = self.steps - s
        if s == 0:
            send_left, send_right = self.part(away)
        else:
            near_left = self.part(count - away).astype(F32)
            near_right = self.part(away).astype(F32)
            if s == 1:
                half = near_left.shape[0] // 2
                send_left = jnp.concatenate(
                    [near_left[:half] + self.left.astype(F32), near_left[half:]], 0
                )
                send_right = jnp.concatenate(
                    [near_right[:half], near_right[half:] + self.right.astype(F32)], 0
                )
            else:
                send_left = near_left + self.left.astype(F32)
                send_right = near_right + self.right.astype(F32)
        send_left, send_right = send_left.astype(BF), send_right.astype(BF)
        if after is not None:
            after, send_left, send_right = tied(after, send_left, send_right)
        self.left = ring_hop(send_left, count, -1)
        self.right = ring_hop(send_right, count, 1)
        self.done += 1
        return after

    def tie(self, value):
        value, self.right, self.left = tied(value, self.right, self.left)
        return value

    def finish(self):
        return self.part(0).astype(F32) + self.right.astype(F32) + self.left.astype(F32)


MESH_ID = pl.DeviceIdType.MESH
DEEP = 4


class Spot:
    def __init__(self):
        e, f = lax.axis_index("expert"), lax.axis_index("fsdp")
        self.x, self.c = e // 2, lax.rem(e, 2)
        self.z, self.y = f // 2, lax.rem(f, 2)
        self.ox, self.oy, self.oc = 1 - self.x, 1 - self.y, 1 - self.c

    def place(self, x=None, y=None, z=None, c=None):
        x = self.x if x is None else x
        y = self.y if y is None else y
        z = self.z if z is None else z
        c = self.c if c is None else c
        return {"expert": x * 2 + c, "fsdp": z * 2 + y}

    def block(self, x, y, z, c):
        return (x * 2 + c) * 8 + z * 2 + y

    def greet(self):
        barrier = pltpu.get_barrier_semaphore()
        for target in (self.place(x=self.ox), self.place(y=self.oy), self.place(c=self.oc)):
            pl.semaphore_signal(barrier, inc=1, device_id=target, device_id_type=MESH_ID)
        for step in (-1, 1):

            @pl.when(self.inside(self.z + step))
            def _(step=step):
                pl.semaphore_signal(
                    barrier, inc=1, device_id=self.along(step), device_id_type=MESH_ID
                )

        pl.semaphore_wait(barrier, 4 + self.z * (DEEP - 1 - self.z) // 2)

    def wrap(self, step):
        return lax.rem(self.z + step + DEEP, DEEP)

    def along(self, step):
        return self.place(z=self.wrap(step))

    def inside(self, z):
        return (z >= 0) & (z < DEEP)


def dense_gather_kernel(cut, x_ref, out_ref, send_sems, recv_sems, own_sem):
    me = Spot()
    rows = x_ref.shape[0]
    spans = [(0, cut), (cut, rows - cut)]
    pending = []

    def view(ref, h):
        return ref.at[pl.ds(*spans[h])]

    def send(src, blk, h, target, cond):
        copy = pltpu.make_async_remote_copy(
            src_ref=src,
            dst_ref=view(out_ref.at[blk], h),
            send_sem=send_sems.at[len(pending)],
            recv_sem=recv_sems.at[blk, h],
            device_id=target,
            device_id_type=MESH_ID,
        )
        pending.append((copy, cond))
        if cond is None:
            copy.start()
        else:
            pl.when(cond)(copy.start)

    def arrive(blk, h, cond):
        copy = pltpu.make_async_remote_copy(
            src_ref=view(out_ref.at[blk], h),
            dst_ref=view(out_ref.at[blk], h),
            send_sem=send_sems.at[0],
            recv_sem=recv_sems.at[blk, h],
            device_id=me.place(c=me.oc),
            device_id_type=MESH_ID,
        )
        if cond is None:
            copy.wait_recv()
        else:
            pl.when(cond)(copy.wait_recv)

    def both(a, b):
        return b if a is None else (a if b is None else a & b)

    by_y, by_x = me.place(y=me.oy), me.place(x=me.ox)
    core = me.place(c=me.oc)
    me.greet()
    mine = me.block(me.x, me.y, me.z, me.c)
    own = pltpu.make_async_copy(x_ref, out_ref.at[mine], own_sem)
    own.start()
    for h in range(2):
        for step in (-1, 1):
            send(view(x_ref, h), mine, h, me.along(step), me.inside(me.z + step))
    for h in range(2):
        for target in (by_y, by_x, core):
            send(view(x_ref, h), mine, h, target, None)

    def line(dist):
        if dist == 0:
            return [(me.z, None, 0)]
        return [(me.wrap(s * dist), me.inside(me.z + s * dist), s) for s in (-1, 1)]

    def from_line(dist):
        for zb, cond, sign in line(dist):
            blk = me.block(me.x, me.y, zb, me.c)
            for h in range(2):
                arrive(blk, h, cond)
                src = view(out_ref.at[blk], h)
                send(src, blk, h, me.along(-sign), both(cond, me.inside(me.z - sign)))
                for target in (by_y, by_x, core):
                    send(src, blk, h, target, cond)

    def from_side(dist):
        for zb, cond, _ in line(dist):
            for h in range(2):
                one = me.block(me.x, me.oy, zb, me.c)
                two = me.block(me.ox, me.y, zb, me.c)
                onward, last = ((one, by_x), two) if h == 0 else ((two, by_y), one)
                arrive(onward[0], h, cond)
                src = view(out_ref.at[onward[0]], h)
                send(src, onward[0], h, onward[1], cond)
                send(src, onward[0], h, core, cond)
                arrive(last, h, cond)
                send(view(out_ref.at[last], h), last, h, core, cond)

    def from_corner(dist):
        for zb, cond, _ in line(dist):
            blk = me.block(me.ox, me.oy, zb, me.c)
            for h in range(2):
                arrive(blk, h, cond)
                send(view(out_ref.at[blk], h), blk, h, core, cond)

    for dist in range(DEEP):
        if dist > 0:
            from_line(dist)
        from_side(dist)
        if dist > 0:
            from_corner(dist - 1)
    from_corner(DEEP - 1)
    for x in range(2):
        for y in range(2):
            for z in range(DEEP):
                for h in range(2):
                    arrive(me.block(x, y, z, me.oc), h, None)
    own.wait()
    for copy, cond in pending:
        if cond is None:
            copy.wait_send()
        else:
            pl.when(cond)(copy.wait_send)


def dense_gather(x, count):
    rows = x.shape[0]
    if count != 32 or lax.axis_size("fsdp") != 2 * DEEP:
        return lax.all_gather(x, ("expert", "fsdp"), axis=0, tiled=False)
    cut = rows // 32 * 16 + 16 * (rows // 16 % 2)
    return pl.pallas_call(
        functools.partial(dense_gather_kernel, cut),
        out_shape=jax.ShapeDtypeStruct((count,) + x.shape, x.dtype),
        in_specs=[pl.BlockSpec(memory_space=pltpu.VMEM)],
        out_specs=pl.BlockSpec(memory_space=pl.ANY),
        scratch_shapes=[
            pltpu.SemaphoreType.DMA((128,)),
            pltpu.SemaphoreType.DMA((count, 2)),
            pltpu.SemaphoreType.DMA,
        ],
        compiler_params=pltpu.CompilerParams(collective_id=0, has_side_effects=True),
        cost_estimate=pl.CostEstimate(
            flops=0, bytes_accessed=100 * 10**6, transcendentals=0
        ),
        name="dense_gather",
    )(x)


def add_into(dst, src):
    def body(i, _):
        at = pl.ds(pl.multiple_of(i * 16, 16), 16)
        dst[at, :] = (dst[at, :].astype(F32) + src[at, :].astype(F32)).astype(BF)
        return 0

    lax.fori_loop(0, dst.shape[0] // 16, body, 0)


def dense_sum_kernel(
    cut, g_ref, out_ref, acc, cbuf, xbuf, ybuf, zbuf, send_sems, recv_sems, load_sems
):
    me = Spot()
    rows = out_ref.shape[0]
    top, low = pl.ds(0, cut), pl.ds(cut, rows - cut)
    pending = []

    def send(src, dst, at, target, cond=None):
        copy = pltpu.make_async_remote_copy(
            src_ref=src,
            dst_ref=dst,
            send_sem=send_sems.at[len(pending)],
            recv_sem=recv_sems.at[at],
            device_id=target,
            device_id_type=MESH_ID,
        )
        pending.append((copy, cond))
        if cond is None:
            copy.start()
        else:
            pl.when(cond)(copy.start)

    def arrive(dst, at):
        pltpu.make_async_remote_copy(
            src_ref=dst,
            dst_ref=dst,
            send_sem=send_sems.at[0],
            recv_sem=recv_sems.at[at],
            device_id=me.place(c=me.oc),
            device_id_type=MESH_ID,
        ).wait_recv()

    by_y, by_x, core = me.place(y=me.oy), me.place(x=me.ox), me.place(c=me.oc)
    me.greet()
    zs = (0, 3, 2, 1)
    loads = []
    for k in range(DEEP):
        for x in range(2):
            at = x * DEEP + k
            theirs = (x * 2 + me.oc) * 8 + zs[k] * 2
            send(g_ref.at[pl.ds(theirs, 2)], cbuf.at[at], at, core)
            ours = (x * 2 + me.c) * 8 + zs[k] * 2
            load = pltpu.make_async_copy(g_ref.at[pl.ds(ours, 2)], acc.at[at], load_sems.at[at])
            load.start()
            loads.append(load)

    def first(k):
        for x in range(2):
            at = x * DEEP + k
            loads[k * 2 + x].wait()
            arrive(cbuf.at[at], at)
            for y in range(2):
                add_into(acc.at[at, y], cbuf.at[at, y])
        base = 8 + k * 6
        for y in range(2):
            send(acc.at[me.ox * DEEP + k, y, top], xbuf.at[k, y, top], base + y, by_x)
        for x in range(2):
            send(acc.at[x * DEEP + k, me.oy, low], ybuf.at[k, x, low], base + 2 + x, by_y)

    def second(k):
        base = 8 + k * 6
        for y in range(2):
            arrive(xbuf.at[k, y, top], base + y)
            add_into(acc.at[me.x * DEEP + k, y, top], xbuf.at[k, y, top])
        for x in range(2):
            arrive(ybuf.at[k, x, low], base + 2 + x)
            add_into(acc.at[x * DEEP + k, me.y, low], ybuf.at[k, x, low])
        send(acc.at[me.x * DEEP + k, me.oy, top], ybuf.at[k, 0, top], base + 4, by_y)
        send(acc.at[me.ox * DEEP + k, me.y, low], xbuf.at[k, 0, low], base + 5, by_x)

    def third(k):
        base = 8 + k * 6
        block = acc.at[me.x * DEEP + k, me.y]
        arrive(ybuf.at[k, 0, top], base + 4)
        add_into(block.at[top], ybuf.at[k, 0, top])
        arrive(xbuf.at[k, 0, low], base + 5)
        add_into(block.at[low], xbuf.at[k, 0, low])

    def along(k, sign, behind):
        zo = zs[k]
        here = behind if sign > 0 else DEEP - 1 - behind
        term = acc.at[me.x * DEEP + k, me.y]
        base = 32 + k * 4 + (sign + 1)
        side = k * 4 + (sign + 1)
        is_here = me.z == here
        for h, at in ((0, top), (1, low)):
            if behind > 0:

                @pl.when(is_here)
                def _(h=h, at=at):
                    arrive(zbuf.at[side + h, at], base + h)
                    add_into(term.at[at], zbuf.at[side + h, at])

            if here != zo:
                send(
                    term.at[at], zbuf.at[side + h, at], base + h, me.along(sign), is_here
                )

    for step in range(DEEP + 6):
        if step < DEEP:
            first(step)
        if 0 <= step - 1 < DEEP:
            second(step - 1)
        if 0 <= step - 2 < DEEP:
            third(step - 2)
        for k in range(DEEP):
            behind = step - 2 - k
            if behind >= 0:
                if behind <= zs[k]:
                    along(k, 1, behind)
                if behind <= DEEP - 1 - zs[k]:
                    along(k, -1, behind)
    block = acc.at[me.x * DEEP + lax.rem(DEEP - me.z, DEEP), me.y]

    def put(i, _):
        at = pl.ds(pl.multiple_of(i * 16, 16), 16)
        out_ref[at, :] = block[at, :].astype(F32)
        return 0

    lax.fori_loop(0, rows // 16, put, 0)
    for copy, cond in pending:
        if cond is None:
            copy.wait_send()
        else:
            pl.when(cond)(copy.wait_send)


def dense_sum(x):
    count, rows, width = x.shape
    if count != 32 or lax.axis_size("fsdp") != 2 * DEEP:
        flat = x.reshape(count * rows, width)
        return lax.psum_scatter(
            flat, ("expert", "fsdp"), scatter_dimension=0, tiled=True
        ).astype(F32)
    cut = rows // 32 * 16 + 16 * (rows // 16 % 2)
    pair = (2 * DEEP, 2, rows, width)
    return pl.pallas_call(
        functools.partial(dense_sum_kernel, cut),
        out_shape=jax.ShapeDtypeStruct((rows, width), F32),
        in_specs=[pl.BlockSpec(memory_space=pl.ANY)],
        out_specs=pl.BlockSpec(memory_space=pltpu.VMEM),
        scratch_shapes=[
            pltpu.VMEM(pair, BF),
            pltpu.VMEM(pair, BF),
            pltpu.VMEM((DEEP, 2, rows, width), BF),
            pltpu.VMEM((DEEP, 2, rows, width), BF),
            pltpu.VMEM((4 * DEEP, rows, width), BF),
            pltpu.SemaphoreType.DMA((72,)),
            pltpu.SemaphoreType.DMA((48,)),
            pltpu.SemaphoreType.DMA((8,)),
        ],
        compiler_params=pltpu.CompilerParams(
            collective_id=1, has_side_effects=True, vmem_limit_bytes=40 * 1024 * 1024
        ),
        cost_estimate=pl.CostEstimate(
            flops=0, bytes_accessed=100 * 10**6, transcendentals=0
        ),
        name="dense_sum",
    )(x)


SLICE = 256


def gelu_terms(x):
    root = 0.7978845608028654
    square = x * x
    t = jnp.tanh(root * (x + 0.044715 * square * x))
    half = 0.5 * (1.0 + t)
    slope = half + 0.5 * x * (1.0 - t * t) * (root * (1.0 + 3 * 0.044715 * square))
    return x * half, slope


def block_order(count):
    far = count // 2
    order = [far]
    for away in range(1, far + 1):
        order += [k for k in (far - away, far + away) if k < count]
    return order


def chunk_pieces(base, split, ff_shard):
    if not split:
        return [(0, m * ff_shard, m, base, ff_shard) for m in range(3)]
    half = ff_shard // 2
    return [
        (0, 0, 0, base, ff_shard),
        (0, ff_shard, 1, base, half),
        (1, 0, 1, base + half, half),
        (1, half, 2, base, ff_shard),
    ]


def chunk_copies(refs, whole, sems, ff_shard, outward, start=0):
    out = []
    for p, own in enumerate(refs):
        pieces = []
        places = chunk_pieces(p * ff_shard + start, len(own) == 2, ff_shard)
        for n, (src, at, m, row, rows) in enumerate(places):
            block = own[src].at[pl.ds(at, rows)]
            spot = whole.at[m, pl.ds(row, rows)]
            a, b = (spot, block) if outward else (block, spot)
            pieces.append(pltpu.make_async_copy(a, b, sems.at[p, n]))
        out.append(pieces)
    return out


def pair_first(refs):
    return [refs[:2]] + [refs[k : k + 1] for k in range(2, len(refs))]


def fetch_weights(refs, whole, sems, ff_shard, t):
    copies = chunk_copies(pair_first(refs), whole, sems, ff_shard, False)
    ahead = 3

    @pl.when(t == 0)
    def _():
        for pieces in copies[:ahead]:
            for c in pieces:
                c.start()

    for p, pieces in enumerate(copies):
        more = copies[p + ahead] if p + ahead < len(copies) else []

        @pl.when(t == p * ff_shard // SLICE)
        def _(pieces=pieces, more=more):
            for c in more:
                c.start()
            for c in pieces:
                c.wait()


def ffn_forward_kernel(count, ff_shard, rows_ref, *refs):
    chunks, rest = refs[: count + 1], refs[count + 1 :]
    out_ref, act_ref, turn_ref, hid_ref, whole, acc, sems = rest
    t = pl.program_id(0)
    fetch_weights(chunks, whole, sems, ff_shard, t)
    at = pl.ds(pl.multiple_of(t * SLICE, SLICE), SLICE)
    rows = rows_ref[...]
    gate = lax.dot_general(rows, whole[0, at], NT, preferred_element_type=F32)
    up = lax.dot_general(rows, whole[1, at], NT, preferred_element_type=F32)
    act, slope = gelu_terms(gate)
    hidden = (act * up).astype(BF)
    act_ref[0] = act
    turn_ref[0] = up * slope
    hid_ref[0] = hidden
    more = jnp.dot(hidden, whole[2, at], preferred_element_type=F32)

    @pl.when(t == 0)
    def _():
        acc[...] = more

    @pl.when(t > 0)
    def _():
        acc[...] += more

    @pl.when(t == pl.num_programs(0) - 1)
    def _():
        out_ref[...] = acc[...].astype(BF)


def ffn_backward_kernel(count, ff_shard, grad_ref, act_ref, turn_ref, *refs):
    chunks, rest = refs[: count + 1], refs[count + 1 :]
    out_ref, dgate_ref, dup_ref, whole, acc, sems = rest
    t = pl.program_id(0)
    fetch_weights(chunks, whole, sems, ff_shard, t)
    at = pl.ds(pl.multiple_of(t * SLICE, SLICE), SLICE)
    dhid = lax.dot_general(grad_ref[...], whole[2, at], NT, preferred_element_type=F32)
    dgate = (dhid * turn_ref[0]).astype(BF)
    dup = (dhid * act_ref[0]).astype(BF)
    dgate_ref[0] = dgate
    dup_ref[0] = dup
    more = jnp.dot(
        jnp.concatenate([dgate, dup], axis=1),
        jnp.concatenate([whole[0, at], whole[1, at]], axis=0),
        preferred_element_type=F32,
    )

    @pl.when(t == 0)
    def _():
        acc[...] = more

    @pl.when(t > 0)
    def _():
        acc[...] += more

    @pl.when(t == pl.num_programs(0) - 1)
    def _():
        out_ref[...] = acc[...].astype(BF)


def ffn_weights_kernel(
    lead, first, ff_shard, rows_ref, grad_ref, hid_ref, dgate_ref, dup_ref, *refs
):
    chunks, (whole, sems) = refs[:-2], refs[-2:]
    chunks = pair_first(chunks) if lead else [chunks[k : k + 1] for k in range(len(chunks))]
    base = first * ff_shard // SLICE
    t = pl.program_id(0)
    at = pl.ds(pl.multiple_of(t * SLICE, SLICE), SLICE)
    for m, (left, right) in enumerate(
        ((dgate_ref, rows_ref), (dup_ref, rows_ref), (hid_ref, grad_ref))
    ):
        whole[m, at] = lax.dot_general(
            left[0], right[...], TN, preferred_element_type=F32
        ).astype(BF)
    copies = chunk_copies(
        chunks, whole, sems, ff_shard, True, first * ff_shard - base * SLICE
    )
    for p, pieces in enumerate(copies):

        @pl.when(t == ((first + p + 1) * ff_shard - 1) // SLICE - base)
        def _(pieces=pieces):
            for c in pieces:
                c.start()

    @pl.when(t == pl.num_programs(0) - 1)
    def _():
        for pieces in copies:
            for c in pieces:
                c.wait()


def fixed(shape):
    return pl.BlockSpec(shape, lambda t: (0,) * len(shape))


def stepped(shape):
    return pl.BlockSpec(shape, lambda t: (t, 0, 0))


ANY_SPEC = pl.BlockSpec(memory_space=pl.ANY)


def ffn_cost(slots, hidden):
    work = 6 * slots * D * hidden
    return pl.CostEstimate(flops=work, bytes_accessed=40 * 10**6, transcendentals=slots * hidden)


def ffn_params():
    return pltpu.CompilerParams(
        dimension_semantics=("arbitrary",), vmem_limit_bytes=60 * 1024 * 1024
    )


def ffn_forward(rows, chunks, ff_shard):
    slots, count = rows.shape[0], len(chunks) - 1
    hidden = count * ff_shard
    steps = hidden // SLICE
    return pl.pallas_call(
        functools.partial(ffn_forward_kernel, count, ff_shard),
        grid=(steps,),
        out_shape=(
            jax.ShapeDtypeStruct((slots, D), BF),
            jax.ShapeDtypeStruct((steps, slots, SLICE), F32),
            jax.ShapeDtypeStruct((steps, slots, SLICE), F32),
            jax.ShapeDtypeStruct((steps, slots, SLICE), BF),
        ),
        in_specs=[fixed((slots, D))] + [ANY_SPEC] * (count + 1),
        out_specs=(
            fixed((slots, D)),
            stepped((1, slots, SLICE)),
            stepped((1, slots, SLICE)),
            stepped((1, slots, SLICE)),
        ),
        scratch_shapes=[
            pltpu.VMEM((3, hidden, D), BF),
            pltpu.VMEM((slots, D), F32),
            pltpu.SemaphoreType.DMA((count, 4)),
        ],
        compiler_params=ffn_params(),
        cost_estimate=ffn_cost(slots, hidden),
        name="ffn_forward",
    )(rows, *chunks)


def ffn_backward(grad, act, turn, chunks, ff_shard):
    slots, count = grad.shape[0], len(chunks) - 1
    hidden = count * ff_shard
    steps = hidden // SLICE
    tile = jax.ShapeDtypeStruct((steps, slots, SLICE), BF)
    return pl.pallas_call(
        functools.partial(ffn_backward_kernel, count, ff_shard),
        grid=(steps,),
        out_shape=(jax.ShapeDtypeStruct((slots, D), BF), tile, tile),
        in_specs=[fixed((slots, D))]
        + [stepped((1, slots, SLICE))] * 2
        + [ANY_SPEC] * (count + 1),
        out_specs=(fixed((slots, D)),) + (stepped((1, slots, SLICE)),) * 2,
        scratch_shapes=[
            pltpu.VMEM((3, hidden, D), BF),
            pltpu.VMEM((slots, D), F32),
            pltpu.SemaphoreType.DMA((count, 4)),
        ],
        compiler_params=ffn_params(),
        cost_estimate=ffn_cost(slots, hidden),
        name="ffn_backward",
    )(grad, act, turn, *chunks)


def ffn_weights(rows, grad, hid, dgate, dup, first, last, ff_shard):
    slots = rows.shape[0]
    lead = first == 0
    base, end = first * ff_shard // SLICE, -(-last * ff_shard // SLICE)
    full = jax.ShapeDtypeStruct((3 * ff_shard, D), BF)
    half = jax.ShapeDtypeStruct((3 * ff_shard // 2, D), BF)
    shapes = ([half] * 2 if lead else [full]) + [full] * (last - first - 1)
    tile = pl.BlockSpec((1, slots, SLICE), lambda t: (t + base, 0, 0))
    return pl.pallas_call(
        functools.partial(ffn_weights_kernel, lead, first, ff_shard),
        grid=(end - base,),
        out_shape=tuple(shapes),
        in_specs=[fixed((slots, D))] * 2 + [tile] * 3,
        out_specs=(ANY_SPEC,) * len(shapes),
        scratch_shapes=[
            pltpu.VMEM((3, (end - base) * SLICE, D), BF),
            pltpu.SemaphoreType.DMA((last - first, 4)),
        ],
        compiler_params=ffn_params(),
        cost_estimate=ffn_cost(slots, (end - base) * SLICE),
    )(rows, grad, hid, dgate, dup)


def norm_inverse(x):
    return lax.rsqrt(jnp.mean(x * x, axis=-1, keepdims=True) + EPSILON)


def qkv_forward_kernel(x_ref, scale_ref, wq_ref, wk_ref, wv_ref, out_ref, normed_ref):
    @pl.when(pl.program_id(0) == 0)
    def _():
        x = x_ref[...].astype(F32)
        normed_ref[...] = (x * norm_inverse(x) * scale_ref[...]).astype(BF)

    normed = normed_ref[...]
    for c, w in enumerate((wq_ref, wk_ref, wv_ref)):
        y = jnp.dot(normed, w[...].reshape(D, TILE), preferred_element_type=F32).astype(BF)
        for s in range(2):
            out_ref[s, :, c * HALF : (c + 1) * HALF] = y[:, s * HALF : (s + 1) * HALF]


def qkv_forward(x, scale, gathered, shard):
    tokens = x.shape[0]
    count = D // HALF
    weight = [
        pl.BlockSpec((D // shard, shard, TILE), lambda j, c=c: (0, c, j)) for c in range(3)
    ]
    whole = pl.BlockSpec((tokens, D), lambda j: (0, 0))
    return pl.pallas_call(
        qkv_forward_kernel,
        grid=(count // 2,),
        out_shape=(
            jax.ShapeDtypeStruct((count, tokens, 3 * HALF), BF),
            jax.ShapeDtypeStruct((tokens, D), BF),
        ),
        in_specs=[whole, pl.BlockSpec((1, D), lambda j: (0, 0))] + weight,
        out_specs=(pl.BlockSpec((2, tokens, 3 * HALF), lambda j: (j, 0, 0)), whole),
        compiler_params=ffn_params(),
        cost_estimate=pl.CostEstimate(
            flops=6 * tokens * D * D, bytes_accessed=10 * 10**6, transcendentals=0
        ),
        name="qkv_forward",
    )(x, scale, gathered, gathered, gathered)


def qkv_backward_kernel(
    dq_ref, normed_ref, w_ref, x_ref, scale_ref, mid_ref, kept_ref, pack_ref, gin_ref, gain_ref,
    turned, acc,
):
    step = pl.program_id(0) * pl.num_programs(1) + pl.program_id(1)
    dq = jnp.concatenate([dq_ref[0], dq_ref[1]], axis=1)

    @pl.when(step == 0)
    def _():
        turned[...] = transpose_low(normed_ref[...])

    weights = jnp.dot(turned[...], dq, preferred_element_type=F32).astype(BF)
    pack_ref[...] = weights.reshape(pack_ref.shape)
    more = lax.dot_general(dq, w_ref[...].reshape(D, TILE), NT, preferred_element_type=F32)

    @pl.when(step == 0)
    def _():
        acc[...] = more

    @pl.when(step > 0)
    def _():
        acc[...] += more

    @pl.when(step == pl.num_programs(0) * pl.num_programs(1) - 1)
    def _():
        x = x_ref[...].astype(F32)
        inverse = norm_inverse(x)
        grad = acc[...]
        scaled = grad * scale_ref[...]
        inner = jnp.mean(x * scaled, axis=-1, keepdims=True)
        gin_ref[...] = mid_ref[...] + inverse * scaled - x * (inverse * inverse * inverse * inner)
        gain_ref[...] = jnp.broadcast_to(
            jnp.sum(grad * (x * inverse), axis=0, keepdims=True), gain_ref.shape
        )


def qkv_backward(dq, normed, gathered, x, scale, middle, kept, shard):
    tokens = x.shape[0]
    count = D // HALF
    whole = pl.BlockSpec((tokens, D), lambda j, c: (0, 0))
    weight = pl.BlockSpec((D // shard, shard, TILE), lambda j, c: (0, c, j))
    return pl.pallas_call(
        qkv_backward_kernel,
        grid=(count // 2, 3),
        out_shape=(
            jax.ShapeDtypeStruct(kept.shape, BF),
            jax.ShapeDtypeStruct((tokens, D), F32),
            jax.ShapeDtypeStruct((8, D), F32),
        ),
        in_specs=[
            pl.BlockSpec((2, tokens, HALF), lambda j, c: (j, 0, c)),
            whole,
            weight,
            whole,
            pl.BlockSpec((1, D), lambda j, c: (0, 0)),
            whole,
            ANY_SPEC,
        ],
        out_specs=(weight, whole, pl.BlockSpec((8, D), lambda j, c: (0, 0))),
        scratch_shapes=[pltpu.VMEM((D, tokens), BF), pltpu.VMEM((tokens, D), F32)],
        input_output_aliases={6: 0},
        compiler_params=pltpu.CompilerParams(
            dimension_semantics=("arbitrary", "arbitrary"), vmem_limit_bytes=40 * 1024 * 1024
        ),
        cost_estimate=pl.CostEstimate(
            flops=12 * tokens * D * D, bytes_accessed=25 * 10**6, transcendentals=0
        ),
        name="qkv_backward",
    )(dq, normed, gathered, x, scale, middle, kept)


def local(
    inputs,
    w_qkv,
    w_out,
    attn_gain,
    moe_gain,
    w_router,
    bias_table,
    w_gate,
    w_up,
    w_down,
    routes,
    slot_order,
    group_map,
    buckets,
    grad_output,
):
    tok_count = inputs.shape[0]
    expert_count = w_router.shape[1]
    capacity = (5 * TOPK * tok_count + 4 * expert_count - 1) // (4 * expert_count)
    fsdp_count = lax.axis_size("fsdp")
    fsdp_place = lax.axis_index("fsdp")
    expert_place = lax.axis_index("expert")
    group_count = lax.axis_size("expert") * fsdp_count
    sh = Shape(fsdp_count)
    prompt_rows = sh.part * G_LINE
    slot_total = expert_count * capacity
    shard = w_qkv.shape[0]
    ff_shard = w_down.shape[1]

    def by_prompt(x):
        head = x[:prompt_rows].reshape(sh.part, G_LINE, -1).transpose(1, 0, 2)
        return jnp.concatenate([head.reshape(prompt_rows, -1), x[prompt_rows:]], 0)

    def by_token(x):
        head = x[:prompt_rows].reshape(G_LINE, sh.part, -1).transpose(1, 0, 2)
        return jnp.concatenate([head.reshape(prompt_rows, -1), x[prompt_rows:]], 0)

    own_weights = jnp.concatenate([w_gate[0].T, w_up[0].T, w_down[0]], 0)
    spread = [fsdp_count // 8] * 4
    spread[0] += fsdp_count // 2 - sum(spread)

    def run(ring, count):
        for _ in range(count):
            ring.step()

    small = jnp.concatenate(
        [attn_gain, moe_gain, w_router.reshape(-1), bias_table, group_map.astype(BF)]
    )
    small_rows = -(-small.shape[0] // D)
    small_rows = -(-small_rows // 16) * 16
    small = jnp.pad(small, (0, small_rows * D - small.shape[0])).reshape(small_rows, D)
    pack = jnp.concatenate([w_qkv[:, i * D : (i + 1) * D] for i in range(3)] + [w_out, small], 0)
    gathered = dense_gather(pack, group_count)
    own_weights, tail = tied(own_weights, gathered[:, 4 * shard])
    weights = RingGather(own_weights, fsdp_count)
    run(weights, spread[0])
    fused = sh.width == HALF
    out_full = gathered[:, 3 * shard : 4 * shard].reshape(D, D)
    marks = [0, shard, 2 * shard, 2 * shard + shard * expert_count]
    marks += [marks[-1] + bias_table.shape[0]]
    attn_scale = tail[:, marks[0] : marks[1]].reshape(D).astype(F32)
    moe_scale = tail[:, marks[1] : marks[2]].reshape(D).astype(F32)
    router = tail[:, marks[2] : marks[3]].reshape(D, expert_count).astype(F32)
    table = tail[:, marks[3] : marks[4]].reshape(fsdp_count, sh.hp, BUCKETS)
    my_table = lax.dynamic_index_in_dim(table, fsdp_place, 0, keepdims=False).astype(F32)
    groups = tail[:, marks[4]].reshape(-1, fsdp_count)
    my_groups = lax.dynamic_index_in_dim(groups, expert_place, 0, keepdims=False)
    my_groups = my_groups.astype(jnp.int32)
    bucket = buckets.reshape(SPAN_BLOCKS, HALF)

    token_input = by_prompt(inputs)
    grad_rows_low = by_prompt(grad_output)
    routes = by_prompt(routes)
    slot_order = by_prompt(slot_order)

    input_float = token_input.astype(F32)
    if fused:
        by_heads, normed_low = qkv_forward(token_input, attn_scale[None, :], gathered, shard)
    else:
        qkv_full = jnp.concatenate(
            [gathered[:, i * shard : (i + 1) * shard].reshape(D, D) for i in range(3)], 1
        )
        normed, first_pull = jax.vjp(rms_scale, input_float, attn_scale)
        normed_low = normed.astype(BF)
        qkv_rows = jnp.dot(normed_low, qkv_full, preferred_element_type=F32).astype(BF)
        by_heads = (
            qkv_rows.reshape(tok_count, 3, fsdp_count, sh.width)
            .transpose(2, 0, 1, 3)
            .reshape(fsdp_count, tok_count, 3 * sh.width)
        )
    head_qkv = lax.all_to_all(by_heads, "fsdp", split_axis=0, concat_axis=0, tiled=True)
    run(weights, spread[1])
    head_qkv = weights.tie(head_qkv)
    head_att, att_turned, att_lse = attend_forward(sh, my_groups, my_table, bucket, head_qkv)
    att_back = lax.all_to_all(head_att, "fsdp", split_axis=0, concat_axis=0, tiled=True)
    run(weights, spread[2])
    att_back = weights.tie(att_back)
    run(weights, spread[3])
    attn_low = att_back.transpose(1, 0, 2).reshape(tok_count, D)

    middle = input_float + jnp.dot(attn_low, out_full, preferred_element_type=F32)
    second_normed, second_pull = jax.vjp(rms_scale, middle, moe_scale)
    (gate_pair, losses), router_pull = jax.vjp(
        lambda normed_rows, router_rows: route_local(normed_rows, router_rows, routes),
        second_normed,
        router,
    )
    kept_mask = (slot_order < capacity).astype(F32)
    gate_kept = gate_pair * kept_mask
    slot_ids = jnp.arange(slot_total, dtype=jnp.int32)
    slot_place = jnp.where(slot_order < capacity, routes * capacity + slot_order, -1)
    hot = [slot_place[:, k : k + 1] == slot_ids[None, :] for k in range(TOPK)]
    any_low = (hot[0] | hot[1]).astype(BF)
    outgoing = lax.dot_general(
        any_low, second_normed.astype(BF), TN, preferred_element_type=F32
    ).astype(BF)

    def swap_experts(rows):
        rows = rows.reshape(expert_count, capacity, D)
        rows = lax.all_to_all(rows, "expert", split_axis=0, concat_axis=0, tiled=True)
        return rows.reshape(slot_total, D)

    expert_rows = swap_experts(outgoing)
    slot_gate = jnp.sum(
        jnp.where(hot[0], gate_kept[:, 0:1], 0.0) + jnp.where(hot[1], gate_kept[:, 1:2], 0.0),
        axis=0,
    )
    slot_grad = lax.dot_general(any_low, grad_rows_low, TN, preferred_element_type=F32)
    grad_result = swap_experts((slot_gate[:, None] * slot_grad).astype(BF))

    order = block_order(fsdp_count)
    far = order[0]
    blocks = list(weights.chunks[far]) + [weights.chunks[k] for k in order[1:]]
    result_rows, act, turn, hidden = ffn_forward(expert_rows, blocks, ff_shard)
    returned = swap_experts(result_rows)
    grad_rows, grad_gate_pre, grad_up_pre = ffn_backward(
        grad_result, act, turn, blocks, ff_shard
    )
    grad_sent = swap_experts(grad_rows)
    halves = (expert_rows, grad_result, hidden, grad_gate_pre, grad_up_pre)
    early = ffn_weights(*halves, 0, 3, ff_shard)
    late = ffn_weights(*halves, 3, fsdp_count, ff_shard)
    totals = dict(zip(order[1:], early[2:] + late))
    totals[far] = early[:2]

    def part(k):
        return totals[k]

    sums = RingScatter(part, fsdp_count)
    run(sums, spread[0])

    picked = [
        jnp.dot(h.astype(BF), returned, preferred_element_type=F32) for h in hot
    ]
    block_out = middle + gate_kept[:, 0:1] * picked[0] + gate_kept[:, 1:2] * picked[1]
    output = by_token(block_out.astype(BF))
    grad_final = grad_rows_low.astype(F32)
    grad_pair = (
        jnp.stack([jnp.sum(grad_final * p, axis=-1) for p in picked], -1) * kept_mask
    )
    grad_second = jnp.dot(any_low, grad_sent, preferred_element_type=F32)
    loss_weights = jnp.array([ZLOSS_FACTOR, BALANCE_FACTOR], F32) / group_count
    router_normed, grad_router = router_pull((grad_pair, loss_weights))
    grad_middle_part, grad_moe_gain = second_pull(grad_second + router_normed)
    grad_middle = grad_final + grad_middle_part
    grad_branch = grad_middle.astype(BF)
    grad_attn = lax.dot_general(grad_branch, out_full, NT, preferred_element_type=F32)
    grad_attn = grad_attn.astype(BF)
    head_grad = (
        grad_attn.reshape(tok_count, fsdp_count, sh.width).transpose(1, 0, 2)
    )
    head_grad = lax.all_to_all(head_grad, "fsdp", split_axis=0, concat_axis=0, tiled=True)
    run(sums, spread[1])
    head_grad = sums.tie(head_grad)
    head_dqkv, head_table = attend_backward(
        sh, my_groups, my_table, bucket, head_qkv, head_grad, att_turned, att_lse
    )
    run(sums, spread[2])
    head_dqkv = sums.tie(head_dqkv)
    back_dqkv = lax.all_to_all(head_dqkv, "fsdp", split_axis=0, concat_axis=0, tiled=True)
    sums.step()
    run(sums, spread[3] - 1)
    expert_sums = sums.finish()
    grad_gate = expert_sums[:ff_shard].T
    grad_up = expert_sums[ff_shard : 2 * ff_shard].T
    grad_down = expert_sums[2 * ff_shard :]
    grad_out_w = lax.dot_general(attn_low, grad_branch, TN, preferred_element_type=F32)

    def rows_of(x):
        return x.astype(BF).reshape(group_count, shard, -1)

    place_table = (jnp.arange(fsdp_count) == fsdp_place).astype(F32)
    whole_table = place_table[:, None] * head_table[:, 0][None, :]
    if fused:
        kept = jnp.pad(rows_of(grad_out_w), ((0, 0), (3 * shard, small_rows), (0, 0)))
        kept, grad_inputs, gains = qkv_backward(
            back_dqkv, normed_low, gathered, token_input, attn_scale[None, :], grad_middle, kept,
            shard,
        )
        grad_attn_gain = gains[0]
    else:
        grad_qkv = (
            back_dqkv.reshape(fsdp_count, tok_count, 3, sh.width)
            .transpose(1, 2, 0, 3)
            .reshape(tok_count, 3 * D)
        )
        grad_qkv_w = lax.dot_general(normed_low, grad_qkv, TN, preferred_element_type=F32)
        grad_normed = lax.dot_general(grad_qkv, qkv_full, NT, preferred_element_type=F32)
        grad_input_part, grad_attn_gain = first_pull(grad_normed)
        grad_inputs = grad_middle + grad_input_part
        parts = [rows_of(grad_qkv_w[:, i * D : (i + 1) * D]) for i in range(3)]
        kept = jnp.concatenate(parts + [rows_of(grad_out_w)], 1)
        kept = jnp.pad(kept, ((0, 0), (0, small_rows), (0, 0)))
    smalls = [grad_attn_gain, grad_moe_gain, grad_router, whole_table.reshape(-1)]
    smalls = jnp.concatenate([p.astype(BF).reshape(group_count, -1) for p in smalls], 1)
    smalls = jnp.pad(smalls, ((0, 0), (0, small_rows * D - smalls.shape[1])))
    smalls = smalls.reshape(group_count, small_rows, D)
    sums_dense = dense_sum(lax.dynamic_update_slice(kept, smalls, (0, 4 * shard, 0)))
    grad_inputs = by_token(grad_inputs)
    sum_qkv = jnp.concatenate([sums_dense[i * shard : (i + 1) * shard] for i in range(3)], 1)
    sum_out = sums_dense[3 * shard : 4 * shard]
    sum_small = sums_dense[4 * shard]
    sum_attn = sum_small[marks[0] : marks[1]]
    sum_moe = sum_small[marks[1] : marks[2]]
    sum_router = sum_small[marks[2] : marks[3]].reshape(shard, expert_count)
    sum_table = sum_small[marks[3] : marks[4]]
    return (
        output,
        losses[None, :],
        grad_inputs,
        sum_qkv,
        sum_out,
        sum_attn,
        sum_moe,
        sum_router,
        sum_table,
        grad_gate[None],
        grad_up[None],
        grad_down[None],
    )


def solution(mesh):
    rows = P(("expert", "fsdp"), None)
    flat = P(("expert", "fsdp"))
    cols = P("expert", None, "fsdp")
    deep = P("expert", "fsdp", None)
    in_specs = (
        rows, rows, rows, flat, flat, rows, flat, cols, cols, deep, rows, rows, flat, P(), rows,
    )
    out_specs = (rows, rows, rows, rows, rows, flat, flat, rows, flat, cols, cols, deep)

    return jax.shard_map(local, mesh=mesh, in_specs=in_specs, out_specs=out_specs, check_vma=False)
```

profile of v0, /device:TPU:11, one launch (start us, length us, event | category | flops | bytes accessed | tf_op | source)
XLA Modules:
  0.0 775.3 jit_solution(61010682438982830)
XLA Ops:
  8.4 49.2 %dense_gather.1.wq_ref.wk_ref.wv_ref.w_ref = bf16[32,144,1024]{2,1,0:T(8,128)(2,1)} custom-call(bf16[144,1024]{1,0:T(8,128)(2,1)} %copy-done.34), custom_call_target="tpu_custom_call" | custom-call | bytes 100000000 | tf_op jit(solution)/shard_map/dense_gather/pallas_call | solution.py:769
  65.1 6.9 qkv_forward.1
  72.0 5.3 all-to-all-start
  77.3 32.6 %collective-permute-done.refs_7_ = bf16[1056,1024]{1,0:T(8,128)(2,1)} collective-permute-done((bf16[1056,1024]{1,0:T(8,128)(2,1)}, bf16[1056,1024]{1,0:T(8,128)(2,1)}, u32[]{:S(2)}, u32[]{:S(2)}) %collective-permute-start) | collective-permute-done | bytes 2162720 | tf_op jit(solution)/shard_map/ppermute | solution.py:526
  112.0 49.1 %all-to-all-done.x_ref = bf16[8,384,384]{2,1,0:T(8,128)(2,1)S(1)} async-done(((bf16[8,384,384]{2,1,0:T(8,128)(2,1)}), bf16[8,384,384]{2,1,0:T(8,128)(2,1)S(1)}, u32[]{:S(2)}, u32[]{:S(2)}) %all-to-all-start) | async-done | bytes 2359328 | tf_op jit(solution)/shard_map/all_to_all | solution.py:1422
  161.1 46.3 %collective-permute-done.1.refs_5_ = bf16[1056,1024]{1,0:T(8,128)(2,1)} collective-permute-done((bf16[1056,1024]{1,0:T(8,128)(2,1)}, bf16[1056,1024]{1,0:T(8,128)(2,1)}, u32[]{:S(2)}, u32[]{:S(2)}) %collective-permute-start.1) | collective-permute-done | bytes 2162720 | tf_op jit(solution)/shard_map/ppermute | solution.py:526
  210.3 23.1 %attend_forward.1 = (bf16[8,384,128]{2,1,0:T(8,128)(2,1)}, f32[12,128,256]{2,1,0:T(8,128)S(1)}, f32[12,8,256]{2,1,0:T(8,128)S(1)}) custom-call(s32[8]{0:T(128)S(1)} %fusion.49.group_ref, f32[2,32]{1,0:T(2,128)S(1)} %fusion.51.table_ref, s32[9,128]{1,0:T(8,128)S(1)} %bitcast.87, bf16[8,384,384]{2,1,0:T(8,128)(2,1)S(1)} %all-to-all-done.x_ref), custom_call_target="tpu_custom_call" | custom-call | flops 10000000000 | bytes 8000000 | tf_op jit(solution)/shard_map/attend_forward/pallas_call | solution.py:465
  234.5 3.6 all-to-all-start.1
  238.9 3.3 slice.176
  245.2 27.2 %all-to-all-done.1 = bf16[8,384,128]{2,1,0:T(8,128)(2,1)S(1)} async-done(((bf16[8,384,128]{2,1,0:T(8,128)(2,1)}), bf16[8,384,128]{2,1,0:T(8,128)(2,1)S(1)}, u32[]{:S(2)}, u32[]{:S(2)}) %all-to-all-start.1) | async-done | bytes 786464 | tf_op jit(solution)/shard_map/all_to_all | solution.py:1426
  272.8 3.0 multiply_reduce_fusion.2
  275.8 2.6 convolution_convert_fusion.1
  278.4 6.6 all-to-all-start.2
  285.0 2.3 slice.188
  288.8 2.3 slice.189
  295.5 2.5 multiply_convert_fusion
  298.0 9.5 %all-to-all-done.2 = bf16[4,240,1024]{2,1,0:T(8,128)(2,1)} async-done(((bf16[4,240,1024]{2,1,0:T(8,128)(2,1)}), bf16[4,240,1024]{2,1,0:T(8,128)(2,1)}, u32[]{:S(2)}, u32[]{:S(2)}) %all-to-all-start.2) | async-done | bytes 1966112 | tf_op jit(solution)/shard_map/all_to_all | solution.py:1451
  307.5 6.2 all-to-all-start.4
  316.9 34.6 %ffn_forward.1 = (bf16[960,1024]{1,0:T(8,128)(2,1)}, f32[11,960,256]{2,1,0:T(8,128)}, f32[11,960,256]{2,1,0:T(8,128)}, bf16[11,960,256]{2,1,0:T(8,128)(2,1)}) custom-call(bf16[960,1024]{1,0:T(8,128)(2,1)} %bitcast.18.rows_ref, bf16[528,1024]{1,0:T(8,128)(2,1)} %collective-permute-done.6.refs_0_, bf16[528,1024]{1,0:T(8,128)(2,1)} %collective-permute-done.7.refs_1_, ...), custom_call_target="tpu_custom_call" | custom-call | flops 16609443840 | bytes 40000000 | tf_op jit(solution)/shard_map/ffn_forward/pallas_call | solution.py:1145
  351.6 5.7 all-to-all-start.3
  357.3 39.7 %ffn_backward.1 = (bf16[960,1024]{1,0:T(8,128)(2,1)}, bf16[11,960,256]{2,1,0:T(8,128)(2,1)}, bf16[11,960,256]{2,1,0:T(8,128)(2,1)}) custom-call(bf16[960,1024]{1,0:T(8,128)(2,1)} %bitcast.31.grad_ref, f32[11,960,256]{2,1,0:T(8,128)} %get-tuple-element.63.act_ref, f32[11,960,256]{2,1,0:T(8,128)} %get-tuple-element.64.turn_ref, ...), custom_call_target="tpu_custom_call" | custom-call | flops 16609443840 | bytes 40000000 | tf_op jit(solution)/shard_map/ffn_backward/pallas_call | solution.py:1177
  397.0 13.8 %shard_map.247 = (bf16[528,1024]{1,0:T(8,128)(2,1)}, bf16[528,1024]{1,0:T(8,128)(2,1)}, bf16[1056,1024]{1,0:T(8,128)(2,1)}, bf16[1056,1024]{1,0:T(8,128)(2,1)}) custom-call(bf16[960,1024]{1,0:T(8,128)(2,1)} %bitcast.18.rows_ref, bf16[960,1024]{1,0:T(8,128)(2,1)} %bitcast.31.grad_ref, bf16[11,960,256]{2,1,0:T(8,128)(2,1)} %get-tuple-element.66.hid_ref, ...), custom_call_target="tpu_custom_call" | custom-call | flops 7549747200 | bytes 40000000 | tf_op jit(solution)/shard_map/pallas_call | solution.py:1204
  413.6 2.4 slice.195
  417.0 19.4 %collective-permute-done.8 = bf16[528,1024]{1,0:T(8,128)(2,1)S(1)} collective-permute-done((bf16[528,1024]{1,0:T(8,128)(2,1)}, bf16[528,1024]{1,0:T(8,128)(2,1)S(1)}, u32[]{:S(2)}, u32[]{:S(2)}) %collective-permute-start.8) | collective-permute-done | bytes 1081376 | tf_op jit(solution)/shard_map/ppermute | solution.py:526
  436.8 5.5 all-to-all-start.5
  442.3 2.9 pad_maximum_fusion.1
  450.3 2.6 fusion.6
  453.0 4.3 fusion.4
  457.3 7.5 all-to-all-done.5
  464.9 2.6 fusion.16
  473.9 4.9 all-to-all-start.6
  478.8 17.8 %shard_map.248 = (bf16[1056,1024]{1,0:T(8,128)(2,1)}, bf16[1056,1024]{1,0:T(8,128)(2,1)}, bf16[1056,1024]{1,0:T(8,128)(2,1)}, bf16[1056,1024]{1,0:T(8,128)(2,1)}, bf16[1056,1024]{1,0:T(8,128)(2,1)}) custom-call(bf16[960,1024]{1,0:T(8,128)(2,1)} %bitcast.18.rows_ref, bf16[960,1024]{1,0:T(8,128)(2,1)} %bitcast.31.grad_ref, ...), custom_call_target="tpu_custom_call" | custom-call | flops 10569646080 | bytes 40000000 | tf_op jit(solution)/shard_map/pallas_call | solution.py:1204
  496.6 14.4 %all-to-all-done.6.do_ref = bf16[8,384,128]{2,1,0:T(8,128)(2,1)S(1)} async-done(((bf16[8,384,128]{2,1,0:T(8,128)(2,1)}), bf16[8,384,128]{2,1,0:T(8,128)(2,1)S(1)}, u32[]{:S(2)}, u32[]{:S(2)}) %all-to-all-start.6) | async-done | bytes 786464 | tf_op jit(solution)/shard_map/all_to_all | solution.py:1503
  511.0 3.4 add_convert_fusion.3
  514.4 3.5 collective-permute-start.12
  518.0 2.7 add_convert_fusion.2
  522.7 43.1 %attend_backward.1 = (bf16[8,384,384]{2,1,0:T(8,128)(2,1)S(1)}, f32[64,128]{1,0:T(8,128)S(1)}) custom-call(s32[8]{0:T(128)S(1)} %fusion.49.group_ref, f32[2,32]{1,0:T(2,128)S(1)} %fusion.51.table_ref, s32[9,128]{1,0:T(8,128)S(1)} %bitcast.88, bf16[8,384,384]{2,1,0:T(8,128)(2,1)} %copy-done.2, bf16[8,384,128]{2,1,0:T(8,128)(2,1)S(1)} %all-to-all-done.6.do_ref, ...), custom_call_target="tpu_custom_call" | custom-call | flops 20000000000 | bytes 12000000 | tf_op jit(solution)/shard_map/attend_backward/pallas_call | solution.py:490
  567.3 6.6 all-to-all-start.7
  573.9 4.8 add_convert_fusion
  578.8 4.0 add_convert_fusion.1
  588.0 2.6 convolution_convert_fusion
  590.6 6.6 pad.13.kept_ref
  601.2 69.3 %collective-permute-done.15 = bf16[1056,1024]{1,0:T(8,128)(2,1)} collective-permute-done((bf16[1056,1024]{1,0:T(8,128)(2,1)}, bf16[1056,1024]{1,0:T(8,128)(2,1)}, u32[]{:S(2)}, u32[]{:S(2)}) %collective-permute-start.15) | collective-permute-done | bytes 2162720 | tf_op jit(solution)/shard_map/ppermute | solution.py:526
  671.4 4.4 convert_add_fusion
  675.8 2.2 slice_bitcast_fusion
  678.0 15.6 %qkv_backward.1 = (bf16[32,144,1024]{2,1,0:T(8,128)(2,1)}, f32[384,1024]{1,0:T(8,128)S(1)}, f32[8,1024]{1,0:T(8,128)S(1)}) custom-call(bf16[8,384,384]{2,1,0:T(8,128)(2,1)} %all-to-all-done.7.dq_ref, bf16[384,1024]{1,0:T(8,128)(2,1)S(1)} %copy-done.4, bf16[32,144,1024]{2,1,0:T(8,128)(2,1)} %dense_gather.1.wq_ref.wk_ref.wv_ref.w_ref, ...), custom_call_target="tpu_custom_call", output_to_operand_aliasing={{0}: (6, {})} | custom-call | flops 4831838208 | bytes 25000000 | tf_op jit(solution)/shard_map/qkv_backward/pallas_call | solution.py:1301
  695.6 3.7 copy-done
  699.3 69.6 %dense_sum.1 = f32[144,1024]{1,0:T(8,128)S(1)} custom-call(bf16[32,144,1024]{2,1,0:T(8,128)(2,1)S(1)} %copy-done), custom_call_target="tpu_custom_call" | custom-call | bytes 100000000 | tf_op jit(solution)/shard_map/dense_sum/pallas_call | solution.py:933
  (282 shorter events, 69.7 us)
Async XLA Ops:
  8.4 51.0 %copy-start.31 = (bf16[1,352,1024]{2,1,0:T(8,128)(2,1)S(1)}, bf16[1,352,1024]{2,1,0:T(8,128)(2,1)}, u32[]{:S(2)}) copy-start(bf16[1,352,1024]{2,1,0:T(8,128)(2,1)} %param.25) | copy-start | bytes 2162692
  8.4 51.0 %copy-start.32 = (bf16[1,1024,352]{1,2,0:T(8,128)(2,1)S(1)}, bf16[1,1024,352]{1,2,0:T(8,128)(2,1)}, u32[]{:S(2)}) copy-start(bf16[1,1024,352]{1,2,0:T(8,128)(2,1)} %param.24) | copy-start | bytes 2162692
  8.4 51.0 %copy-start.33 = (bf16[1,1024,352]{1,2,0:T(8,128)(2,1)S(1)}, bf16[1,1024,352]{1,2,0:T(8,128)(2,1)}, u32[]{:S(2)}) copy-start(bf16[1,1024,352]{1,2,0:T(8,128)(2,1)} %param.23) | copy-start | bytes 2162692
  60.9 48.9 %collective-permute-start = (bf16[1056,1024]{1,0:T(8,128)(2,1)}, bf16[1056,1024]{1,0:T(8,128)(2,1)}, u32[]{:S(2)}, u32[]{:S(2)}) collective-permute-start(bf16[1056,1024]{1,0:T(8,128)(2,1)} %pad_maximum_fusion.refs_8_), channel_id=1, source_target_pairs={{0,2},{2,4},{4,6},{6,7},{7,5},{5,3},{3,1},{1,0},{8,10},{10,12},{12... | collective-permute-start | bytes 6488072 | tf_op jit(solution)/shard_map/ppermute | solution.py:526
  62.2 49.3 %collective-permute-start.2 = (bf16[1056,1024]{1,0:T(8,128)(2,1)}, bf16[1056,1024]{1,0:T(8,128)(2,1)}, u32[]{:S(2)}, u32[]{:S(2)}) collective-permute-start(bf16[1056,1024]{1,0:T(8,128)(2,1)} %pad_maximum_fusion.refs_8_), channel_id=1, source_target_pairs={{0,1},{2,0},{4,2},{6,4},{7,6},{5,7},{3,5},{1,3},{8,9},{10,8},{12,1... | collective-permute-start | bytes 6488072 | tf_op jit(solution)/shard_map/ppermute | solution.py:526
  63.3 8.6 %copy-start.14 = (bf16[128,2,1024]{2,0,1:T(8,128)(2,1)}, bf16[128,2,1024]{2,0,1:T(8,128)(2,1)S(1)}, u32[]{:S(2)}) copy-start(bf16[128,2,1024]{2,0,1:T(8,128)(2,1)S(1)} %copy.49) | copy-start | bytes 1572868
  72.0 138.3 %copy-start.6 = (s32[1152]{0:T(1024)S(1)}, s32[1152]{0:T(1024)}, u32[]{:S(2)}) copy-start(s32[1152]{0:T(1024)} %param.29) | copy-start | bytes 13828
  72.0 89.2 %all-to-all-start = ((bf16[8,384,384]{2,1,0:T(8,128)(2,1)}), bf16[8,384,384]{2,1,0:T(8,128)(2,1)S(1)}, u32[]{:S(2)}, u32[]{:S(2)}) async-start(bf16[8,384,384]{2,1,0:T(8,128)(2,1)} %get-tuple-element.53), calls=%async_computation | async-start | bytes 4718592 | tf_op jit(solution)/shard_map/all_to_all | solution.py:1422
  109.9 97.6 %collective-permute-start.1 = (bf16[1056,1024]{1,0:T(8,128)(2,1)}, bf16[1056,1024]{1,0:T(8,128)(2,1)}, u32[]{:S(2)}, u32[]{:S(2)}) collective-permute-start(bf16[1056,1024]{1,0:T(8,128)(2,1)} %collective-permute-done.refs_7_), channel_id=1, source_target_pairs={{0,2},{2,4},{4,6},{6,7},{7,5},{5,3},{3,1},{1,0},{8,10},{10,12},{12... | collective-permute-start | bytes 6488072 | tf_op jit(solution)/shard_map/ppermute | solution.py:526
  111.5 97.2 %collective-permute-start.3 = (bf16[1056,1024]{1,0:T(8,128)(2,1)}, bf16[1056,1024]{1,0:T(8,128)(2,1)}, u32[]{:S(2)}, u32[]{:S(2)}) collective-permute-start(bf16[1056,1024]{1,0:T(8,128)(2,1)} %collective-permute-done.2.refs_6_), channel_id=1, source_target_pairs={{0,1},{2,0},{4,2},{6,4},{7,6},{5,7},{3,5},{1,3},{8,9},{10,8},{12,1... | collective-permute-start | bytes 6488072 | tf_op jit(solution)/shard_map/ppermute | solution.py:526
  161.1 72.2 %copy-start.2 = (bf16[8,384,384]{2,1,0:T(8,128)(2,1)}, bf16[8,384,384]{2,1,0:T(8,128)(2,1)S(1)}, u32[]{:S(2)}) copy-start(bf16[8,384,384]{2,1,0:T(8,128)(2,1)S(1)} %all-to-all-done.x_ref) | copy-start | bytes 7077892
  208.8 63.6 %collective-permute-start.4 = (bf16[1056,1024]{1,0:T(8,128)(2,1)}, bf16[1056,1024]{1,0:T(8,128)(2,1)}, u32[]{:S(2)}, u32[]{:S(2)}) collective-permute-start(bf16[1056,1024]{1,0:T(8,128)(2,1)} %collective-permute-done.1.refs_5_), channel_id=1, source_target_pairs={{0,2},{2,4},{4,6},{6,7},{7,5},{5,3},{3,1},{1,0},{8,10},{10,12},{12... | collective-permute-start | bytes 6488072 | tf_op jit(solution)/shard_map/ppermute | solution.py:526
  209.7 62.7 %collective-permute-start.5 = (bf16[1056,1024]{1,0:T(8,128)(2,1)}, bf16[1056,1024]{1,0:T(8,128)(2,1)}, u32[]{:S(2)}, u32[]{:S(2)}) collective-permute-start(bf16[1056,1024]{1,0:T(8,128)(2,1)} %collective-permute-done.3.refs_4_), channel_id=1, source_target_pairs={{0,1},{2,0},{4,2},{6,4},{7,6},{5,7},{3,5},{1,3},{8,9},{10,8},{12,1... | collective-permute-start | bytes 6488072 | tf_op jit(solution)/shard_map/ppermute | solution.py:526
  234.5 37.9 %all-to-all-start.1 = ((bf16[8,384,128]{2,1,0:T(8,128)(2,1)}), bf16[8,384,128]{2,1,0:T(8,128)(2,1)S(1)}, u32[]{:S(2)}, u32[]{:S(2)}) async-start(bf16[8,384,128]{2,1,0:T(8,128)(2,1)} %get-tuple-element.56), calls=%async_computation.1 | async-start | bytes 1572864 | tf_op jit(solution)/shard_map/all_to_all | solution.py:1426
  242.2 30.6 %copy-start.58 = (s32[128,2]{0,1:T(2,128)}, s32[128,2]{0,1:T(2,128)S(1)}, u32[]{:S(2)}) copy-start(s32[128,2]{0,1:T(2,128)S(1)} %slice.178) | copy-start | bytes 3076
  242.5 30.4 %copy-start.15 = (bf16[128,2,1024]{2,0,1:T(8,128)(2,1)S(1)}, bf16[128,2,1024]{2,0,1:T(8,128)(2,1)}, u32[]{:S(2)}) copy-start(bf16[128,2,1024]{2,0,1:T(8,128)(2,1)} %copy-done.14) | copy-start | bytes 1572868
  243.5 226.2 %copy-start.38 = (f32[1024]{0:T(1024)}, f32[1024]{0:T(1024)S(1)}, u32[]{:S(2)}) copy-start(f32[1024]{0:T(1024)S(1)} %reshape.270) | copy-start | bytes 12292
  245.2 30.6 %copy-start.64 = (s32[384]{0:T(512)}, s32[384]{0:T(512)S(1)}, u32[]{:S(2)}) copy-start(s32[384]{0:T(512)S(1)} %get-tuple-element.142) | copy-start | bytes 4612
  245.2 30.7 %copy-start.66 = (s32[384]{0:T(512)}, s32[384]{0:T(512)S(1)}, u32[]{:S(2)}) copy-start(s32[384]{0:T(512)S(1)} %get-tuple-element.143) | copy-start | bytes 4612
  275.8 193.9 %copy-start.9 = (f32[384,1024]{1,0:T(8,128)}, f32[384,1024]{1,0:T(8,128)S(1)}, u32[]{:S(2)}) copy-start(f32[384,1024]{1,0:T(8,128)S(1)} %get-tuple-element.167) | copy-start | bytes 4718596
  275.8 193.9 %copy-start.42 = (f32[384]{0:T(512)}, f32[384]{0:T(512)S(1)}, u32[]{:S(2)}) copy-start(f32[384]{0:T(512)S(1)} %fusion.43) | copy-start | bytes 4612
  278.4 29.1 %all-to-all-start.2 = ((bf16[4,240,1024]{2,1,0:T(8,128)(2,1)}), bf16[4,240,1024]{2,1,0:T(8,128)(2,1)}, u32[]{:S(2)}, u32[]{:S(2)}) async-start(bf16[4,240,1024]{2,1,0:T(8,128)(2,1)} %bitcast.107), calls=%async_computation.2 | async-start | bytes 3932160 | tf_op jit(solution)/shard_map/all_to_all | solution.py:1451
  287.3 7.6 copy-start.48
  287.3 7.6 copy-start.50
  287.3 7.8 %copy-start.59 = (s32[128,2]{0,1:T(2,128)S(1)}, s32[128,2]{0,1:T(2,128)}, u32[]{:S(2)}) copy-start(s32[128,2]{0,1:T(2,128)} %copy-done.58) | copy-start | bytes 3076
  287.3 7.8 %copy-start.65 = (s32[384]{0:T(512)S(1)}, s32[384]{0:T(512)}, u32[]{:S(2)}) copy-start(s32[384]{0:T(512)} %copy-done.64) | copy-start | bytes 4612
  287.3 7.8 %copy-start.67 = (s32[384]{0:T(512)S(1)}, s32[384]{0:T(512)}, u32[]{:S(2)}) copy-start(s32[384]{0:T(512)} %copy-done.66) | copy-start | bytes 4612
  287.3 8.2 %copy-start.25 = (bf16[128,2,1024]{2,0,1:T(8,128)(2,1)S(1)}, bf16[128,2,1024]{2,0,1:T(8,128)(2,1)}, u32[]{:S(2)}) copy-start(bf16[128,2,1024]{2,0,1:T(8,128)(2,1)} %copy.55) | copy-start | bytes 1572868
  287.3 8.2 %copy-start.28 = (bf16[128,1024]{1,0:T(8,128)(2,1)S(1)}, bf16[128,1024]{1,0:T(8,128)(2,1)}, u32[]{:S(2)}) copy-start(bf16[128,1024]{1,0:T(8,128)(2,1)} %slice.194) | copy-start | bytes 786436
  287.3 27.5 %collective-permute-start.6 = (bf16[528,1024]{1,0:T(8,128)(2,1)}, bf16[528,1024]{1,0:T(8,128)(2,1)}, u32[]{:S(2)}, u32[]{:S(2)}) collective-permute-start(bf16[528,1024]{1,0:T(8,128)(2,1)} %slice.188), channel_id=1, source_target_pairs={{0,2},{2,4},{4,6},{6,7},{7,5},{5,3},{3,1},{1,0},{8,10},{10,12},{12... | collective-permute-start | bytes 3244040 | tf_op jit(solution)/shard_map/ppermute | solution.py:526
  291.1 25.8 %collective-permute-start.7 = (bf16[528,1024]{1,0:T(8,128)(2,1)}, bf16[528,1024]{1,0:T(8,128)(2,1)}, u32[]{:S(2)}, u32[]{:S(2)}) collective-permute-start(bf16[528,1024]{1,0:T(8,128)(2,1)} %slice.189), channel_id=1, source_target_pairs={{0,1},{2,0},{4,2},{6,4},{7,6},{5,7},{3,5},{1,3},{8,9},{10,8},{12,1... | collective-permute-start | bytes 3244040 | tf_op jit(solution)/shard_map/ppermute | solution.py:526
  294.1 173.7 %copy-start.35 = (f32[384,4]{0,1:T(4,128)}, f32[384,4]{0,1:T(4,128)S(1)}, u32[]{:S(2)}) copy-start(f32[384,4]{0,1:T(4,128)S(1)} %get-tuple-element.169) | copy-start | bytes 18436
  294.2 173.7 %copy-start.44 = (f32[384]{0:T(512)}, f32[384]{0:T(512)S(1)}, u32[]{:S(2)}) copy-start(f32[384]{0:T(512)S(1)} %is-finite_select_fusion) | copy-start | bytes 4612
  307.5 44.1 %all-to-all-start.4 = ((bf16[4,240,1024]{2,1,0:T(8,128)(2,1)}), bf16[4,240,1024]{2,1,0:T(8,128)(2,1)}, u32[]{:S(2)}, u32[]{:S(2)}) async-start(bf16[4,240,1024]{2,1,0:T(8,128)(2,1)} %bitcast.108), calls=%async_computation.4 | async-start | bytes 3932160 | tf_op jit(solution)/shard_map/all_to_all | solution.py:1451
  351.6 85.2 %all-to-all-start.3 = ((bf16[4,240,1024]{2,1,0:T(8,128)(2,1)}), bf16[4,240,1024]{2,1,0:T(8,128)(2,1)}, u32[]{:S(2)}, u32[]{:S(2)}) async-start(bf16[4,240,1024]{2,1,0:T(8,128)(2,1)} %bitcast.106), calls=%async_computation.3 | async-start | bytes 3932160 | tf_op jit(solution)/shard_map/all_to_all | solution.py:1451
  410.9 25.5 %collective-permute-start.8 = (bf16[528,1024]{1,0:T(8,128)(2,1)}, bf16[528,1024]{1,0:T(8,128)(2,1)S(1)}, u32[]{:S(2)}, u32[]{:S(2)}) collective-permute-start(bf16[528,1024]{1,0:T(8,128)(2,1)} %get-tuple-element.70), channel_id=1, source_target_pairs={{0,2},{2,4},{4,6},{6,7},{7,5},{5,3},{3,1},{1,0},{8,10},{10,12},{12... | collective-permute-start | bytes 3244040 | tf_op jit(solution)/shard_map/ppermute | solution.py:526
  412.4 34.3 %collective-permute-start.10 = (bf16[528,1024]{1,0:T(8,128)(2,1)}, bf16[528,1024]{1,0:T(8,128)(2,1)}, u32[]{:S(2)}, u32[]{:S(2)}) collective-permute-start(bf16[528,1024]{1,0:T(8,128)(2,1)} %get-tuple-element.72), channel_id=1, source_target_pairs={{0,1},{2,0},{4,2},{6,4},{7,6},{5,7},{3,5},{1,3},{8,9},{10,8},{12,1... | collective-permute-start | bytes 3244040 | tf_op jit(solution)/shard_map/ppermute | solution.py:526
  416.0 20.4 %copy-start.22 = (bf16[1056,1024]{1,0:T(8,128)(2,1)S(1)}, bf16[1056,1024]{1,0:T(8,128)(2,1)}, u32[]{:S(2)}) copy-start(bf16[1056,1024]{1,0:T(8,128)(2,1)} %get-tuple-element.69) | copy-start | bytes 6488068
  436.8 28.0 %all-to-all-start.5 = ((bf16[4,240,1024]{2,1,0:T(8,128)(2,1)}), bf16[4,240,1024]{2,1,0:T(8,128)(2,1)}, u32[]{:S(2)}, u32[]{:S(2)}) async-start(bf16[4,240,1024]{2,1,0:T(8,128)(2,1)} %bitcast.105), calls=%async_computation.5 | async-start | bytes 3932160 | tf_op jit(solution)/shard_map/all_to_all | solution.py:1451
  445.2 65.8 %collective-permute-start.9 = (bf16[1056,1024]{1,0:T(8,128)(2,1)}, bf16[1056,1024]{1,0:T(8,128)(2,1)}, u32[]{:S(2)}, u32[]{:S(2)}) collective-permute-start(bf16[1056,1024]{1,0:T(8,128)(2,1)} %pad_maximum_fusion.1), channel_id=1, source_target_pairs={{0,2},{2,4},{4,6},{6,7},{7,5},{5,3},{3,1},{1,0},{8,10},{10,12},{12... | collective-permute-start | bytes 6488072 | tf_op jit(solution)/shard_map/ppermute | solution.py:526
  450.0 61.1 %collective-permute-start.11 = (bf16[1056,1024]{1,0:T(8,128)(2,1)}, bf16[1056,1024]{1,0:T(8,128)(2,1)}, u32[]{:S(2)}, u32[]{:S(2)}) collective-permute-start(bf16[1056,1024]{1,0:T(8,128)(2,1)} %pad_maximum_fusion.2), channel_id=1, source_target_pairs={{0,1},{2,0},{4,2},{6,4},{7,6},{5,7},{3,5},{1,3},{8,9},{10,8},{12,1... | collective-permute-start | bytes 6488072 | tf_op jit(solution)/shard_map/ppermute | solution.py:526
  473.9 37.1 %all-to-all-start.6 = ((bf16[8,384,128]{2,1,0:T(8,128)(2,1)}), bf16[8,384,128]{2,1,0:T(8,128)(2,1)S(1)}, u32[]{:S(2)}, u32[]{:S(2)}) async-start(bf16[8,384,128]{2,1,0:T(8,128)(2,1)} %bitcast.35), calls=%async_computation.6 | async-start | bytes 1572864 | tf_op jit(solution)/shard_map/all_to_all | solution.py:1503
  514.4 52.8 %collective-permute-start.12 = (bf16[1056,1024]{1,0:T(8,128)(2,1)S(1)}, bf16[1056,1024]{1,0:T(8,128)(2,1)}, u32[]{:S(2)}, u32[]{:S(2)}) collective-permute-start(bf16[1056,1024]{1,0:T(8,128)(2,1)S(1)} %add_convert_fusion.3), channel_id=1, source_target_pairs={{0,2},{2,4},{4,6},{6,7},{7,5},{5,3},{3,1},{1,0},{8,10},{10,12},{12... | collective-permute-start | bytes 6488072 | tf_op jit(solution)/shard_map/ppermute | solution.py:526
  520.7 46.6 %collective-permute-start.13 = (bf16[1056,1024]{1,0:T(8,128)(2,1)S(1)}, bf16[1056,1024]{1,0:T(8,128)(2,1)}, u32[]{:S(2)}, u32[]{:S(2)}) collective-permute-start(bf16[1056,1024]{1,0:T(8,128)(2,1)S(1)} %add_convert_fusion.2), channel_id=1, source_target_pairs={{0,1},{2,0},{4,2},{6,4},{7,6},{5,7},{3,5},{1,3},{8,9},{10,8},{12,1... | collective-permute-start | bytes 6488072 | tf_op jit(solution)/shard_map/ppermute | solution.py:526
  567.3 110.7 %all-to-all-start.7 = ((bf16[8,384,384]{2,1,0:T(8,128)(2,1)}), bf16[8,384,384]{2,1,0:T(8,128)(2,1)}, u32[]{:S(2)}, u32[]{:S(2)}) async-start(bf16[8,384,384]{2,1,0:T(8,128)(2,1)} %copy-done.3), calls=%async_computation.7 | async-start | bytes 4718592 | tf_op jit(solution)/shard_map/all_to_all | solution.py:1511
  578.7 91.9 %collective-permute-start.15 = (bf16[1056,1024]{1,0:T(8,128)(2,1)}, bf16[1056,1024]{1,0:T(8,128)(2,1)}, u32[]{:S(2)}, u32[]{:S(2)}) collective-permute-start(bf16[1056,1024]{1,0:T(8,128)(2,1)} %add_convert_fusion), channel_id=1, source_target_pairs={{0,1},{2,0},{4,2},{6,4},{7,6},{5,7},{3,5},{1,3},{8,9},{10,8},{12,1... | collective-permute-start | bytes 6488072 | tf_op jit(solution)/shard_map/ppermute | solution.py:526
  578.8 7.5 copy-start.30
  582.8 88.6 %collective-permute-start.14 = (bf16[1056,1024]{1,0:T(8,128)(2,1)}, bf16[1056,1024]{1,0:T(8,128)(2,1)}, u32[]{:S(2)}, u32[]{:S(2)}) collective-permute-start(bf16[1056,1024]{1,0:T(8,128)(2,1)} %add_convert_fusion.1), channel_id=1, source_target_pairs={{0,2},{2,4},{4,6},{6,7},{7,5},{5,3},{3,1},{1,0},{8,10},{10,12},{12... | collective-permute-start | bytes 6488072 | tf_op jit(solution)/shard_map/ppermute | solution.py:526
  (51 other events, 162.4 us)
where the time goes:
time: 785 us; the launch traced here: 775 us
  Pallas kernels  313 us (40%)
  waiting for transfers between devices  281 us (36%)
  starting transfers between devices  62.9 us (8%)
  local copies, waits for them, and re-layouts  52.3 us (7%)
  other arithmetic  36.7 us (5%)
  matrix products  25.1 us (3%)
    ppermute x16, waiting for transfers between devices, ring_hop(): lax.ppermute(x, 'fsdp', [(ring[i], ring[(i + step) % count]) for i in ran...  173 us
    pallas_call x1, Pallas kernels, dense_sum(): pl.pallas_call(functools.partial(dense_sum_kernel, cut), out_shape=jax.Sh...  69.6 us
    pallas_call x1, Pallas kernels, dense_gather(): pl.pallas_call(functools.partial(dense_gather_kernel, cut), out_shape=jax...  49.2 us
    all_to_all x1, waiting for transfers between devices, local(): lax.all_to_all(by_heads, 'fsdp', split_axis=0, concat_axis=0, tiled=True)  49.1 us
    pallas_call x1, Pallas kernels, attend_backward(): pl.pallas_call(functools.partial(attn_backward_kernel, sh), out_shape=(ja...  43.1 us
    pallas_call x1, Pallas kernels, ffn_backward(): pl.pallas_call(functools.partial(ffn_backward_kernel, count, ff_shard), g...  39.7 us
    pallas_call x1, Pallas kernels, ffn_forward(): pl.pallas_call(functools.partial(ffn_forward_kernel, count, ff_shard), gr...  34.6 us
    pallas_call x2, Pallas kernels, ffn_weights(): pl.pallas_call(functools.partial(ffn_weights_kernel, lead, first, ff_shar...  31.7 us
  transfers between devices with their start and end apart: 24, of which 15 were waited for; matrix products, arithmetic and copies ran while one was open for 10% of the time, Pallas kernels for 23%

commit v1 on v0

--- a/solution.py
+++ b/solution.py
@@ -559,11 +559,6 @@
         else:
             self.chunks[s] = (self.right, self.left)
 
-    def tie(self, value):
-        value, self.right, self.left = tied(value, self.right, self.left)
-        self.keep()
-        return value
-
 
 class RingScatter:
     def __init__(self, part, count):
@@ -1421,11 +1416,9 @@
         )
     head_qkv = lax.all_to_all(by_heads, "fsdp", split_axis=0, concat_axis=0, tiled=True)
     run(weights, spread[1])
-    head_qkv = weights.tie(head_qkv)
     head_att, att_turned, att_lse = attend_forward(sh, my_groups, my_table, bucket, head_qkv)
     att_back = lax.all_to_all(head_att, "fsdp", split_axis=0, concat_axis=0, tiled=True)
     run(weights, spread[2])
-    att_back = weights.tie(att_back)
     run(weights, spread[3])
     attn_low = att_back.transpose(1, 0, 2).reshape(tok_count, D)
 

time: 785 us -> 781 us (level)
    ppermute x16, waiting for transfers between devices: 173 us -> 250 us  [ring_hop(): lax.ppermute(x, 'fsdp', [(ring[i], ring[(i + step) % count]) for i in ran...]
    all_to_all x1, waiting for transfers between devices: 49.1 us -> 0.01 us  [local(): lax.all_to_all(by_heads, 'fsdp', split_axis=0, concat_axis=0, tiled=True)]
    all_to_all x1, waiting for transfers between devices: 27.2 us -> 6.73 us  [local(): lax.all_to_all(head_att, 'fsdp', split_axis=0, concat_axis=0, tiled=True)]
    all_to_all x4, waiting for transfers between devices: 17.1 us -> 7.65 us  [swap_experts(): lax.all_to_all(rows, 'expert', split_axis=0, concat_axis=0, tiled=True)]
  transfers between devices with their start and end apart: 24 -> 24, of which waited for: 15 -> 12; matrix products, arithmetic and copies ran while one was open for 10% -> 11% of each run, Pallas kernels for 23% -> 22%
where the time goes in v1:
time: 781 us; the launch traced here: 771 us
  Pallas kernels  313 us (40%)
  waiting for transfers between devices  279 us (36%)
  starting transfers between devices  66.5 us (9%)
  local copies, waits for them, and re-layouts  46.1 us (6%)
  other arithmetic  36.8 us (5%)
  matrix products  25.1 us (3%)
    ppermute x16, waiting for transfers between devices, ring_hop(): lax.ppermute(x, 'fsdp', [(ring[i], ring[(i + step) % count]) for i in ran...  250 us
    pallas_call x1, Pallas kernels, dense_sum(): pl.pallas_call(functools.partial(dense_sum_kernel, cut), out_shape=jax.Sh...  69.5 us
    pallas_call x1, Pallas kernels, dense_gather(): pl.pallas_call(functools.partial(dense_gather_kernel, cut), out_shape=jax...  49.2 us
    pallas_call x1, Pallas kernels, attend_backward(): pl.pallas_call(functools.partial(attn_backward_kernel, sh), out_shape=(ja...  43.1 us
    pallas_call x1, Pallas kernels, ffn_backward(): pl.pallas_call(functools.partial(ffn_backward_kernel, count, ff_shard), g...  39.7 us
    pallas_call x1, Pallas kernels, ffn_forward(): pl.pallas_call(functools.partial(ffn_forward_kernel, count, ff_shard), gr...  34.7 us
    pallas_call x2, Pallas kernels, ffn_weights(): pl.pallas_call(functools.partial(ffn_weights_kernel, lead, first, ff_shar...  31.6 us
    all_to_all x4, starting transfers between devices, swap_experts(): lax.all_to_all(rows, 'expert', split_axis=0, concat_axis=0, tiled=True)  28.2 us
  transfers between devices with their start and end apart: 24, of which 12 were waited for; matrix products, arithmetic and copies ran while one was open for 11% of the time, Pallas kernels for 22%

profile of v1, /device:TPU:11, one launch (start us, length us, event | category | flops | bytes accessed | tf_op | source)
XLA Modules:
  0.0 770.8 jit_solution(15340944079178144856)
XLA Ops:
  3.7 49.2 %dense_gather.1.wq_ref.wk_ref.wv_ref.w_ref = bf16[32,144,1024]{2,1,0:T(8,128)(2,1)} custom-call(bf16[144,1024]{1,0:T(8,128)(2,1)} %copy-done.33), custom_call_target="tpu_custom_call" | custom-call | bytes 100000000 | tf_op jit(solution)/shard_map/dense_gather/pallas_call | solution.py:764
  57.6 6.9 qkv_forward.1
  64.5 5.3 all-to-all-start
  71.3 97.1 %collective-permute-done.refs_7_ = bf16[1056,1024]{1,0:T(8,128)(2,1)} collective-permute-done((bf16[1056,1024]{1,0:T(8,128)(2,1)}, bf16[1056,1024]{1,0:T(8,128)(2,1)}, u32[]{:S(2)}, u32[]{:S(2)}) %collective-permute-start) | collective-permute-done | bytes 2162720 | tf_op jit(solution)/shard_map/ppermute | solution.py:526
  171.1 23.1 %attend_forward.1 = (bf16[8,384,128]{2,1,0:T(8,128)(2,1)}, f32[12,128,256]{2,1,0:T(8,128)S(1)}, f32[12,8,256]{2,1,0:T(8,128)S(1)}) custom-call(s32[8]{0:T(128)S(1)} %fusion.49.group_ref, f32[2,32]{1,0:T(2,128)S(1)} %fusion.51.table_ref, s32[9,128]{1,0:T(8,128)S(1)} %bitcast.87, bf16[8,384,384]{2,1,0:T(8,128)(2,1)S(1)} %all-to-all-done.x_ref), custom_call_target="tpu_custom_call" | custom-call | flops 10000000000 | bytes 8000000 | tf_op jit(solution)/shard_map/attend_forward/pallas_call | solution.py:465
  195.3 4.1 all-to-all-start.1
  199.4 18.0 %collective-permute-done.1.refs_5_ = bf16[1056,1024]{1,0:T(8,128)(2,1)} collective-permute-done((bf16[1056,1024]{1,0:T(8,128)(2,1)}, bf16[1056,1024]{1,0:T(8,128)(2,1)}, u32[]{:S(2)}, u32[]{:S(2)}) %collective-permute-start.1) | collective-permute-done | bytes 2162720 | tf_op jit(solution)/shard_map/ppermute | solution.py:526
  217.4 2.6 collective-permute-start.2
  220.7 3.3 slice.176
  227.0 6.7 all-to-all-done.1
  234.1 3.0 multiply_reduce_fusion.2
  237.2 2.6 convolution_convert_fusion.1
  239.7 7.7 all-to-all-start.2
  248.5 31.6 %collective-permute-done.2.refs_3_ = bf16[1056,1024]{1,0:T(8,128)(2,1)} collective-permute-done((bf16[1056,1024]{1,0:T(8,128)(2,1)}, bf16[1056,1024]{1,0:T(8,128)(2,1)}, u32[]{:S(2)}, u32[]{:S(2)}) %collective-permute-start.2) | collective-permute-done | bytes 2162720 | tf_op jit(solution)/shard_map/ppermute | solution.py:526
  284.7 2.3 slice.227
  288.4 2.5 multiply_convert_fusion
  290.9 7.1 all-to-all-start.4
  298.0 8.9 %collective-permute-done.3.refs_0_ = bf16[528,1024]{1,0:T(8,128)(2,1)} collective-permute-done((bf16[528,1024]{1,0:T(8,128)(2,1)}, bf16[528,1024]{1,0:T(8,128)(2,1)}, u32[]{:S(2)}, u32[]{:S(2)}) %collective-permute-start.3) | collective-permute-done | bytes 1081376 | tf_op jit(solution)/shard_map/ppermute | solution.py:526
  306.9 4.4 collective-permute-done.7.refs_1_
  311.3 34.7 %ffn_forward.1 = (bf16[960,1024]{1,0:T(8,128)(2,1)}, f32[11,960,256]{2,1,0:T(8,128)}, f32[11,960,256]{2,1,0:T(8,128)}, bf16[11,960,256]{2,1,0:T(8,128)(2,1)}) custom-call(bf16[960,1024]{1,0:T(8,128)(2,1)} %bitcast.18.rows_ref, bf16[528,1024]{1,0:T(8,128)(2,1)} %collective-permute-done.3.refs_0_, bf16[528,1024]{1,0:T(8,128)(2,1)} %collective-permute-done.7.refs_1_, ...), custom_call_target="tpu_custom_call" | custom-call | flops 16609443840 | bytes 40000000 | tf_op jit(solution)/shard_map/ffn_forward/pallas_call | solution.py:1140
  346.0 7.9 %all-to-all-start.3 = ((bf16[4,240,1024]{2,1,0:T(8,128)(2,1)}), bf16[4,240,1024]{2,1,0:T(8,128)(2,1)}, u32[]{:S(2)}, u32[]{:S(2)}) async-start(bf16[4,240,1024]{2,1,0:T(8,128)(2,1)} %bitcast.106), calls=%async_computation.3 | async-start | bytes 3932160 | tf_op jit(solution)/shard_map/all_to_all | solution.py:1444
  353.9 39.7 %ffn_backward.1 = (bf16[960,1024]{1,0:T(8,128)(2,1)}, bf16[11,960,256]{2,1,0:T(8,128)(2,1)}, bf16[11,960,256]{2,1,0:T(8,128)(2,1)}) custom-call(bf16[960,1024]{1,0:T(8,128)(2,1)} %bitcast.31.grad_ref, f32[11,960,256]{2,1,0:T(8,128)} %get-tuple-element.51.act_ref, f32[11,960,256]{2,1,0:T(8,128)} %get-tuple-element.52.turn_ref, ...), custom_call_target="tpu_custom_call" | custom-call | flops 16609443840 | bytes 40000000 | tf_op jit(solution)/shard_map/ffn_backward/pallas_call | solution.py:1172
  393.6 13.8 %shard_map.247 = (bf16[528,1024]{1,0:T(8,128)(2,1)}, bf16[528,1024]{1,0:T(8,128)(2,1)}, bf16[1056,1024]{1,0:T(8,128)(2,1)}, bf16[1056,1024]{1,0:T(8,128)(2,1)}) custom-call(bf16[960,1024]{1,0:T(8,128)(2,1)} %bitcast.18.rows_ref, bf16[960,1024]{1,0:T(8,128)(2,1)} %bitcast.31.grad_ref, bf16[11,960,256]{2,1,0:T(8,128)(2,1)} %get-tuple-element.54.hid_ref, ...), custom_call_target="tpu_custom_call" | custom-call | flops 7549747200 | bytes 40000000 | tf_op jit(solution)/shard_map/pallas_call | solution.py:1199
  410.1 2.4 slice.195
  413.5 19.3 %collective-permute-done.8 = bf16[528,1024]{1,0:T(8,128)(2,1)S(1)} collective-permute-done((bf16[528,1024]{1,0:T(8,128)(2,1)}, bf16[528,1024]{1,0:T(8,128)(2,1)S(1)}, u32[]{:S(2)}, u32[]{:S(2)}) %collective-permute-start.8) | collective-permute-done | bytes 1081376 | tf_op jit(solution)/shard_map/ppermute | solution.py:526
  433.3 5.6 all-to-all-start.5
  438.9 2.9 pad_maximum_fusion.1
  446.8 2.6 fusion.6
  449.4 4.3 fusion.4
  453.7 7.6 all-to-all-done.5
  461.5 2.6 fusion.16
  470.4 3.5 all-to-all-start.6
  473.9 17.8 %shard_map.248 = (bf16[1056,1024]{1,0:T(8,128)(2,1)}, bf16[1056,1024]{1,0:T(8,128)(2,1)}, bf16[1056,1024]{1,0:T(8,128)(2,1)}, bf16[1056,1024]{1,0:T(8,128)(2,1)}, bf16[1056,1024]{1,0:T(8,128)(2,1)}) custom-call(bf16[960,1024]{1,0:T(8,128)(2,1)} %bitcast.18.rows_ref, bf16[960,1024]{1,0:T(8,128)(2,1)} %bitcast.31.grad_ref, ...), custom_call_target="tpu_custom_call" | custom-call | flops 10569646080 | bytes 40000000 | tf_op jit(solution)/shard_map/pallas_call | solution.py:1199
  491.8 14.0 %all-to-all-done.6.do_ref = bf16[8,384,128]{2,1,0:T(8,128)(2,1)S(1)} async-done(((bf16[8,384,128]{2,1,0:T(8,128)(2,1)}), bf16[8,384,128]{2,1,0:T(8,128)(2,1)S(1)}, u32[]{:S(2)}, u32[]{:S(2)}) %all-to-all-start.6) | async-done | bytes 786464 | tf_op jit(solution)/shard_map/all_to_all | solution.py:1496
  505.8 3.4 add_convert_fusion.3
  509.2 4.2 collective-permute-start.12
  513.4 2.7 add_convert_fusion.2
  518.1 43.1 %attend_backward.1 = (bf16[8,384,384]{2,1,0:T(8,128)(2,1)S(1)}, f32[64,128]{1,0:T(8,128)S(1)}) custom-call(s32[8]{0:T(128)S(1)} %fusion.49.group_ref, f32[2,32]{1,0:T(2,128)S(1)} %fusion.51.table_ref, s32[9,128]{1,0:T(8,128)S(1)} %bitcast.88, bf16[8,384,384]{2,1,0:T(8,128)(2,1)} %copy-done.2, bf16[8,384,128]{2,1,0:T(8,128)(2,1)S(1)} %all-to-all-done.6.do_ref, ...), custom_call_target="tpu_custom_call" | custom-call | flops 20000000000 | bytes 12000000 | tf_op jit(solution)/shard_map/attend_backward/pallas_call | solution.py:490
  563.5 5.8 all-to-all-start.7
  569.3 4.8 add_convert_fusion
  574.2 4.0 add_convert_fusion.1
  583.4 2.6 convolution_convert_fusion
  586.1 6.6 pad.13.kept_ref
  596.7 69.3 %collective-permute-done.15 = bf16[1056,1024]{1,0:T(8,128)(2,1)} collective-permute-done((bf16[1056,1024]{1,0:T(8,128)(2,1)}, bf16[1056,1024]{1,0:T(8,128)(2,1)}, u32[]{:S(2)}, u32[]{:S(2)}) %collective-permute-start.15) | collective-permute-done | bytes 2162720 | tf_op jit(solution)/shard_map/ppermute | solution.py:526
  666.9 4.4 convert_add_fusion
  673.5 15.6 %qkv_backward.1 = (bf16[32,144,1024]{2,1,0:T(8,128)(2,1)}, f32[384,1024]{1,0:T(8,128)S(1)}, f32[8,1024]{1,0:T(8,128)S(1)}) custom-call(bf16[8,384,384]{2,1,0:T(8,128)(2,1)} %all-to-all-done.7.dq_ref, bf16[384,1024]{1,0:T(8,128)(2,1)S(1)} %copy-done.4, bf16[32,144,1024]{2,1,0:T(8,128)(2,1)} %dense_gather.1.wq_ref.wk_ref.wv_ref.w_ref, ...), custom_call_target="tpu_custom_call", output_to_operand_aliasing={{0}: (6, {})} | custom-call | flops 4831838208 | bytes 25000000 | tf_op jit(solution)/shard_map/qkv_backward/pallas_call | solution.py:1296
  691.1 3.7 copy-done
  694.8 69.5 %dense_sum.1 = f32[144,1024]{1,0:T(8,128)S(1)} custom-call(bf16[32,144,1024]{2,1,0:T(8,128)(2,1)S(1)} %copy-done), custom_call_target="tpu_custom_call" | custom-call | bytes 100000000 | tf_op jit(solution)/shard_map/dense_sum/pallas_call | solution.py:928
  (290 shorter events, 62.0 us)
Async XLA Ops:
  1.8 54.9 %copy-start.17 = (bf16[128,1024]{1,0:T(8,128)(2,1)}, bf16[128,1024]{1,0:T(8,128)(2,1)S(1)}, u32[]{:S(2)}) copy-start(bf16[128,1024]{1,0:T(8,128)(2,1)S(1)} %slice.168) | copy-start | bytes 786436
  3.7 50.4 %copy-start.30 = (bf16[1,352,1024]{2,1,0:T(8,128)(2,1)S(1)}, bf16[1,352,1024]{2,1,0:T(8,128)(2,1)}, u32[]{:S(2)}) copy-start(bf16[1,352,1024]{2,1,0:T(8,128)(2,1)} %param.25) | copy-start | bytes 2162692
  3.7 50.4 %copy-start.31 = (bf16[1,1024,352]{1,2,0:T(8,128)(2,1)S(1)}, bf16[1,1024,352]{1,2,0:T(8,128)(2,1)}, u32[]{:S(2)}) copy-start(bf16[1,1024,352]{1,2,0:T(8,128)(2,1)} %param.24) | copy-start | bytes 2162692
  3.7 50.4 %copy-start.32 = (bf16[1,1024,352]{1,2,0:T(8,128)(2,1)S(1)}, bf16[1,1024,352]{1,2,0:T(8,128)(2,1)}, u32[]{:S(2)}) copy-start(bf16[1,1024,352]{1,2,0:T(8,128)(2,1)} %param.23) | copy-start | bytes 2162692
  55.9 8.6 %copy-start.14 = (bf16[128,2,1024]{2,0,1:T(8,128)(2,1)}, bf16[128,2,1024]{2,0,1:T(8,128)(2,1)S(1)}, u32[]{:S(2)}) copy-start(bf16[128,2,1024]{2,0,1:T(8,128)(2,1)S(1)} %copy.49) | copy-start | bytes 1572868
  64.5 106.6 %copy-start.6 = (s32[1152]{0:T(1024)S(1)}, s32[1152]{0:T(1024)}, u32[]{:S(2)}) copy-start(s32[1152]{0:T(1024)} %param.29) | copy-start | bytes 13828
  64.5 106.5 %all-to-all-start = ((bf16[8,384,384]{2,1,0:T(8,128)(2,1)}), bf16[8,384,384]{2,1,0:T(8,128)(2,1)S(1)}, u32[]{:S(2)}, u32[]{:S(2)}) async-start(bf16[8,384,384]{2,1,0:T(8,128)(2,1)} %get-tuple-element.47), calls=%async_computation | async-start | bytes 4718592 | tf_op jit(solution)/shard_map/all_to_all | solution.py:1417
  69.8 98.6 %collective-permute-start = (bf16[1056,1024]{1,0:T(8,128)(2,1)}, bf16[1056,1024]{1,0:T(8,128)(2,1)}, u32[]{:S(2)}, u32[]{:S(2)}) collective-permute-start(bf16[1056,1024]{1,0:T(8,128)(2,1)} %pad_maximum_fusion.refs_8_), channel_id=1, source_target_pairs={{0,2},{2,4},{4,6},{6,7},{7,5},{5,3},{3,1},{1,0},{8,10},{10,12},{12... | collective-permute-start | bytes 6488072 | tf_op jit(solution)/shard_map/ppermute | solution.py:526
  71.0 99.6 %collective-permute-start.4 = (bf16[1056,1024]{1,0:T(8,128)(2,1)}, bf16[1056,1024]{1,0:T(8,128)(2,1)}, u32[]{:S(2)}, u32[]{:S(2)}) collective-permute-start(bf16[1056,1024]{1,0:T(8,128)(2,1)} %pad_maximum_fusion.refs_8_), channel_id=1, source_target_pairs={{0,1},{2,0},{4,2},{6,4},{7,6},{5,7},{3,5},{1,3},{8,9},{10,8},{12,1... | collective-permute-start | bytes 6488072 | tf_op jit(solution)/shard_map/ppermute | solution.py:526
  168.4 49.0 %collective-permute-start.1 = (bf16[1056,1024]{1,0:T(8,128)(2,1)}, bf16[1056,1024]{1,0:T(8,128)(2,1)}, u32[]{:S(2)}, u32[]{:S(2)}) collective-permute-start(bf16[1056,1024]{1,0:T(8,128)(2,1)} %collective-permute-done.refs_7_), channel_id=1, source_target_pairs={{0,2},{2,4},{4,6},{6,7},{7,5},{5,3},{3,1},{1,0},{8,10},{10,12},{12... | collective-permute-start | bytes 6488072 | tf_op jit(solution)/shard_map/ppermute | solution.py:526
  170.6 49.4 %collective-permute-start.5 = (bf16[1056,1024]{1,0:T(8,128)(2,1)}, bf16[1056,1024]{1,0:T(8,128)(2,1)}, u32[]{:S(2)}, u32[]{:S(2)}) collective-permute-start(bf16[1056,1024]{1,0:T(8,128)(2,1)} %collective-permute-done.4.refs_6_), channel_id=1, source_target_pairs={{0,1},{2,0},{4,2},{6,4},{7,6},{5,7},{3,5},{1,3},{8,9},{10,8},{12,1... | collective-permute-start | bytes 6488072 | tf_op jit(solution)/shard_map/ppermute | solution.py:526
  171.1 23.1 %copy-start.2 = (bf16[8,384,384]{2,1,0:T(8,128)(2,1)}, bf16[8,384,384]{2,1,0:T(8,128)(2,1)S(1)}, u32[]{:S(2)}) copy-start(bf16[8,384,384]{2,1,0:T(8,128)(2,1)S(1)} %all-to-all-done.x_ref) | copy-start | bytes 7077892
  195.3 24.7 %copy-start.23 = (bf16[384,1024]{1,0:T(8,128)(2,1)S(1)}, bf16[384,1024]{1,0:T(8,128)(2,1)}, u32[]{:S(2)}) copy-start(bf16[384,1024]{1,0:T(8,128)(2,1)} %param.30) | copy-start | bytes 2359300
  195.3 38.4 %all-to-all-start.1 = ((bf16[8,384,128]{2,1,0:T(8,128)(2,1)}), bf16[8,384,128]{2,1,0:T(8,128)(2,1)S(1)}, u32[]{:S(2)}, u32[]{:S(2)}) async-start(bf16[8,384,128]{2,1,0:T(8,128)(2,1)} %get-tuple-element.48), calls=%async_computation.1 | async-start | bytes 1572864 | tf_op jit(solution)/shard_map/all_to_all | solution.py:1420
  217.4 62.7 %collective-permute-start.2 = (bf16[1056,1024]{1,0:T(8,128)(2,1)}, bf16[1056,1024]{1,0:T(8,128)(2,1)}, u32[]{:S(2)}, u32[]{:S(2)}) collective-permute-start(bf16[1056,1024]{1,0:T(8,128)(2,1)} %collective-permute-done.1.refs_5_), channel_id=1, source_target_pairs={{0,2},{2,4},{4,6},{6,7},{7,5},{5,3},{3,1},{1,0},{8,10},{10,12},{12... | collective-permute-start | bytes 6488072 | tf_op jit(solution)/shard_map/ppermute | solution.py:526
  220.0 64.7 %collective-permute-start.6 = (bf16[1056,1024]{1,0:T(8,128)(2,1)}, bf16[1056,1024]{1,0:T(8,128)(2,1)}, u32[]{:S(2)}, u32[]{:S(2)}) collective-permute-start(bf16[1056,1024]{1,0:T(8,128)(2,1)} %collective-permute-done.5.refs_4_), channel_id=1, source_target_pairs={{0,1},{2,0},{4,2},{6,4},{7,6},{5,7},{3,5},{1,3},{8,9},{10,8},{12,1... | collective-permute-start | bytes 6488072 | tf_op jit(solution)/shard_map/ppermute | solution.py:526
  224.0 10.1 %copy-start.58 = (s32[128,2]{0,1:T(2,128)}, s32[128,2]{0,1:T(2,128)S(1)}, u32[]{:S(2)}) copy-start(s32[128,2]{0,1:T(2,128)S(1)} %slice.178) | copy-start | bytes 3076
  224.3 9.8 %copy-start.15 = (bf16[128,2,1024]{2,0,1:T(8,128)(2,1)S(1)}, bf16[128,2,1024]{2,0,1:T(8,128)(2,1)}, u32[]{:S(2)}) copy-start(bf16[128,2,1024]{2,0,1:T(8,128)(2,1)} %copy-done.14) | copy-start | bytes 1572868
  225.3 240.9 %copy-start.37 = (f32[1024]{0:T(1024)}, f32[1024]{0:T(1024)S(1)}, u32[]{:S(2)}) copy-start(f32[1024]{0:T(1024)S(1)} %reshape.270) | copy-start | bytes 12292
  227.0 10.1 %copy-start.64 = (s32[384]{0:T(512)}, s32[384]{0:T(512)S(1)}, u32[]{:S(2)}) copy-start(s32[384]{0:T(512)S(1)} %get-tuple-element.130) | copy-start | bytes 4612
  227.0 10.1 %copy-start.66 = (s32[384]{0:T(512)}, s32[384]{0:T(512)S(1)}, u32[]{:S(2)}) copy-start(s32[384]{0:T(512)S(1)} %get-tuple-element.131) | copy-start | bytes 4612
  237.1 229.1 %copy-start.9 = (f32[384,1024]{1,0:T(8,128)}, f32[384,1024]{1,0:T(8,128)S(1)}, u32[]{:S(2)}) copy-start(f32[384,1024]{1,0:T(8,128)S(1)} %get-tuple-element.155) | copy-start | bytes 4718596
  237.1 229.1 %copy-start.42 = (f32[384]{0:T(512)}, f32[384]{0:T(512)S(1)}, u32[]{:S(2)}) copy-start(f32[384]{0:T(512)S(1)} %fusion.43) | copy-start | bytes 4612
  239.7 51.2 %all-to-all-start.2 = ((bf16[4,240,1024]{2,1,0:T(8,128)(2,1)}), bf16[4,240,1024]{2,1,0:T(8,128)(2,1)}, u32[]{:S(2)}, u32[]{:S(2)}) async-start(bf16[4,240,1024]{2,1,0:T(8,128)(2,1)} %bitcast.107), calls=%async_computation.2 | async-start | bytes 3932160 | tf_op jit(solution)/shard_map/all_to_all | solution.py:1444
  248.4 215.9 %copy-start.34 = (f32[384,4]{0,1:T(4,128)}, f32[384,4]{0,1:T(4,128)S(1)}, u32[]{:S(2)}) copy-start(f32[384,4]{0,1:T(4,128)S(1)} %get-tuple-element.157) | copy-start | bytes 18436
  248.4 215.9 %copy-start.44 = (f32[384]{0:T(512)}, f32[384]{0:T(512)S(1)}, u32[]{:S(2)}) copy-start(f32[384]{0:T(512)S(1)} %is-finite_select_fusion) | copy-start | bytes 4612
  248.5 38.7 %copy-start.56 = (f32[384]{0:T(512)}, f32[384]{0:T(512)S(1)}, u32[]{:S(2)}) copy-start(f32[384]{0:T(512)S(1)} %fusion.37) | copy-start | bytes 4612
  282.4 24.5 %collective-permute-start.3 = (bf16[528,1024]{1,0:T(8,128)(2,1)}, bf16[528,1024]{1,0:T(8,128)(2,1)}, u32[]{:S(2)}, u32[]{:S(2)}) collective-permute-start(bf16[528,1024]{1,0:T(8,128)(2,1)} %slice.226), channel_id=1, source_target_pairs={{0,2},{2,4},{4,6},{6,7},{7,5},{5,3},{3,1},{1,0},{8,10},{10,12},{12... | collective-permute-start | bytes 3244040 | tf_op jit(solution)/shard_map/ppermute | solution.py:526
  287.0 24.3 %collective-permute-start.7 = (bf16[528,1024]{1,0:T(8,128)(2,1)}, bf16[528,1024]{1,0:T(8,128)(2,1)}, u32[]{:S(2)}, u32[]{:S(2)}) collective-permute-start(bf16[528,1024]{1,0:T(8,128)(2,1)} %slice.227), channel_id=1, source_target_pairs={{0,1},{2,0},{4,2},{6,4},{7,6},{5,7},{3,5},{1,3},{8,9},{10,8},{12,1... | collective-permute-start | bytes 3244040 | tf_op jit(solution)/shard_map/ppermute | solution.py:526
  290.9 55.1 %all-to-all-start.4 = ((bf16[4,240,1024]{2,1,0:T(8,128)(2,1)}), bf16[4,240,1024]{2,1,0:T(8,128)(2,1)}, u32[]{:S(2)}, u32[]{:S(2)}) async-start(bf16[4,240,1024]{2,1,0:T(8,128)(2,1)} %bitcast.108), calls=%async_computation.4 | async-start | bytes 3932160 | tf_op jit(solution)/shard_map/all_to_all | solution.py:1444
  346.0 87.3 %all-to-all-start.3 = ((bf16[4,240,1024]{2,1,0:T(8,128)(2,1)}), bf16[4,240,1024]{2,1,0:T(8,128)(2,1)}, u32[]{:S(2)}, u32[]{:S(2)}) async-start(bf16[4,240,1024]{2,1,0:T(8,128)(2,1)} %bitcast.106), calls=%async_computation.3 | async-start | bytes 3932160 | tf_op jit(solution)/shard_map/all_to_all | solution.py:1444
  407.5 25.4 %collective-permute-start.8 = (bf16[528,1024]{1,0:T(8,128)(2,1)}, bf16[528,1024]{1,0:T(8,128)(2,1)S(1)}, u32[]{:S(2)}, u32[]{:S(2)}) collective-permute-start(bf16[528,1024]{1,0:T(8,128)(2,1)} %get-tuple-element.58), channel_id=1, source_target_pairs={{0,2},{2,4},{4,6},{6,7},{7,5},{5,3},{3,1},{1,0},{8,10},{10,12},{12... | collective-permute-start | bytes 3244040 | tf_op jit(solution)/shard_map/ppermute | solution.py:526
  407.6 34.3 %collective-permute-start.10 = (bf16[528,1024]{1,0:T(8,128)(2,1)}, bf16[528,1024]{1,0:T(8,128)(2,1)}, u32[]{:S(2)}, u32[]{:S(2)}) collective-permute-start(bf16[528,1024]{1,0:T(8,128)(2,1)} %get-tuple-element.60), channel_id=1, source_target_pairs={{0,1},{2,0},{4,2},{6,4},{7,6},{5,7},{3,5},{1,3},{8,9},{10,8},{12,1... | collective-permute-start | bytes 3244040 | tf_op jit(solution)/shard_map/ppermute | solution.py:526
  412.5 20.4 %copy-start.22 = (bf16[1056,1024]{1,0:T(8,128)(2,1)S(1)}, bf16[1056,1024]{1,0:T(8,128)(2,1)}, u32[]{:S(2)}) copy-start(bf16[1056,1024]{1,0:T(8,128)(2,1)} %get-tuple-element.57) | copy-start | bytes 6488068
  433.3 28.1 %all-to-all-start.5 = ((bf16[4,240,1024]{2,1,0:T(8,128)(2,1)}), bf16[4,240,1024]{2,1,0:T(8,128)(2,1)}, u32[]{:S(2)}, u32[]{:S(2)}) async-start(bf16[4,240,1024]{2,1,0:T(8,128)(2,1)} %bitcast.105), calls=%async_computation.5 | async-start | bytes 3932160 | tf_op jit(solution)/shard_map/all_to_all | solution.py:1444
  441.8 64.0 %collective-permute-start.9 = (bf16[1056,1024]{1,0:T(8,128)(2,1)}, bf16[1056,1024]{1,0:T(8,128)(2,1)}, u32[]{:S(2)}, u32[]{:S(2)}) collective-permute-start(bf16[1056,1024]{1,0:T(8,128)(2,1)} %pad_maximum_fusion.1), channel_id=1, source_target_pairs={{0,2},{2,4},{4,6},{6,7},{7,5},{5,3},{3,1},{1,0},{8,10},{10,12},{12... | collective-permute-start | bytes 6488072 | tf_op jit(solution)/shard_map/ppermute | solution.py:526
  445.3 60.5 %collective-permute-start.11 = (bf16[1056,1024]{1,0:T(8,128)(2,1)}, bf16[1056,1024]{1,0:T(8,128)(2,1)}, u32[]{:S(2)}, u32[]{:S(2)}) collective-permute-start(bf16[1056,1024]{1,0:T(8,128)(2,1)} %pad_maximum_fusion.2), channel_id=1, source_target_pairs={{0,1},{2,0},{4,2},{6,4},{7,6},{5,7},{3,5},{1,3},{8,9},{10,8},{12,1... | collective-permute-start | bytes 6488072 | tf_op jit(solution)/shard_map/ppermute | solution.py:526
  470.4 35.3 %all-to-all-start.6 = ((bf16[8,384,128]{2,1,0:T(8,128)(2,1)}), bf16[8,384,128]{2,1,0:T(8,128)(2,1)S(1)}, u32[]{:S(2)}, u32[]{:S(2)}) async-start(bf16[8,384,128]{2,1,0:T(8,128)(2,1)} %bitcast.35), calls=%async_computation.6 | async-start | bytes 1572864 | tf_op jit(solution)/shard_map/all_to_all | solution.py:1496
  505.8 7.6 copy-start.19
  509.2 53.4 %collective-permute-start.12 = (bf16[1056,1024]{1,0:T(8,128)(2,1)S(1)}, bf16[1056,1024]{1,0:T(8,128)(2,1)}, u32[]{:S(2)}, u32[]{:S(2)}) collective-permute-start(bf16[1056,1024]{1,0:T(8,128)(2,1)S(1)} %add_convert_fusion.3), channel_id=1, source_target_pairs={{0,2},{2,4},{4,6},{6,7},{7,5},{5,3},{3,1},{1,0},{8,10},{10,12},{12... | collective-permute-start | bytes 6488072 | tf_op jit(solution)/shard_map/ppermute | solution.py:526
  516.1 47.4 %collective-permute-start.13 = (bf16[1056,1024]{1,0:T(8,128)(2,1)S(1)}, bf16[1056,1024]{1,0:T(8,128)(2,1)}, u32[]{:S(2)}, u32[]{:S(2)}) collective-permute-start(bf16[1056,1024]{1,0:T(8,128)(2,1)S(1)} %add_convert_fusion.2), channel_id=1, source_target_pairs={{0,1},{2,0},{4,2},{6,4},{7,6},{5,7},{3,5},{1,3},{8,9},{10,8},{12,1... | collective-permute-start | bytes 6488072 | tf_op jit(solution)/shard_map/ppermute | solution.py:526
  563.5 110.0 %all-to-all-start.7 = ((bf16[8,384,384]{2,1,0:T(8,128)(2,1)}), bf16[8,384,384]{2,1,0:T(8,128)(2,1)}, u32[]{:S(2)}, u32[]{:S(2)}) async-start(bf16[8,384,384]{2,1,0:T(8,128)(2,1)} %copy-done.3), calls=%async_computation.7 | async-start | bytes 4718592 | tf_op jit(solution)/shard_map/all_to_all | solution.py:1504
  574.1 92.0 %collective-permute-start.15 = (bf16[1056,1024]{1,0:T(8,128)(2,1)}, bf16[1056,1024]{1,0:T(8,128)(2,1)}, u32[]{:S(2)}, u32[]{:S(2)}) collective-permute-start(bf16[1056,1024]{1,0:T(8,128)(2,1)} %add_convert_fusion), channel_id=1, source_target_pairs={{0,1},{2,0},{4,2},{6,4},{7,6},{5,7},{3,5},{1,3},{8,9},{10,8},{12,1... | collective-permute-start | bytes 6488072 | tf_op jit(solution)/shard_map/ppermute | solution.py:526
  574.2 7.6 copy-start.29
  578.3 88.6 %collective-permute-start.14 = (bf16[1056,1024]{1,0:T(8,128)(2,1)}, bf16[1056,1024]{1,0:T(8,128)(2,1)}, u32[]{:S(2)}, u32[]{:S(2)}) collective-permute-start(bf16[1056,1024]{1,0:T(8,128)(2,1)} %add_convert_fusion.1), channel_id=1, source_target_pairs={{0,2},{2,4},{4,6},{6,7},{7,5},{5,3},{3,1},{1,0},{8,10},{10,12},{12... | collective-permute-start | bytes 6488072 | tf_op jit(solution)/shard_map/ppermute | solution.py:526
  586.1 6.7 copy-start.43
  586.1 6.7 copy-start.45
  586.1 6.7 copy-start.47
  (55 other events, 173.5 us)

commit v2 on v1

--- a/solution.py
+++ b/solution.py
@@ -951,6 +951,7 @@
 
 
 SLICE = 256
+MARGIN = 2
 
 
 def gelu_terms(x):
@@ -964,10 +965,10 @@
 
 def block_order(count):
     far = count // 2
-    order = [far]
-    for away in range(1, far + 1):
-        order += [k for k in (far - away, far + away) if k < count]
-    return order
+    order = [0]
+    for away in range(1, far):
+        order += [count - away, away]
+    return order + [far]
 
 
 def chunk_pieces(base, split, ff_shard):
@@ -996,12 +997,17 @@
     return out
 
 
-def pair_first(refs):
-    return [refs[:2]] + [refs[k : k + 1] for k in range(2, len(refs))]
-
-
-def fetch_weights(refs, whole, sems, ff_shard, t):
-    copies = chunk_copies(pair_first(refs), whole, sems, ff_shard, False)
+def pair_last(refs):
+    return [refs[k : k + 1] for k in range(len(refs) - 2)] + [refs[-2:]]
+
+
+def single(refs):
+    return [refs[k : k + 1] for k in range(len(refs))]
+
+
+def fetch_weights(blocks, whole, sems, ff_shard, t, first=0, base=0, margin=0):
+    start = first * ff_shard - (base - margin) * SLICE
+    copies = chunk_copies(blocks, whole, sems, ff_shard, False, start)
     ahead = 3
 
     @pl.when(t == 0)
@@ -1013,7 +1019,7 @@
     for p, pieces in enumerate(copies):
         more = copies[p + ahead] if p + ahead < len(copies) else []
 
-        @pl.when(t == p * ff_shard // SLICE)
+        @pl.when(t == max((first + p) * ff_shard // SLICE - base, 0))
         def _(pieces=pieces, more=more):
             for c in more:
                 c.start()
@@ -1021,12 +1027,20 @@
                 c.wait()
 
 
-def ffn_forward_kernel(count, ff_shard, rows_ref, *refs):
-    chunks, rest = refs[: count + 1], refs[count + 1 :]
+def ffn_forward_kernel(count, near, ff_shard, last, rows_ref, *refs):
+    if last:
+        chunks, rest = refs[:3], refs[3:]
+        before_ref, rest = rest[0], rest[4:]
+    else:
+        chunks, rest = refs[: count - 1], refs[count - 1 :]
     out_ref, act_ref, turn_ref, hid_ref, whole, acc, sems = rest
     t = pl.program_id(0)
-    fetch_weights(chunks, whole, sems, ff_shard, t)
-    at = pl.ds(pl.multiple_of(t * SLICE, SLICE), SLICE)
+    if last:
+        fetch_weights(pair_last(chunks), whole, sems, ff_shard, t, count - 2, near, MARGIN)
+        at = pl.ds(pl.multiple_of((t + MARGIN) * SLICE, SLICE), SLICE)
+    else:
+        fetch_weights(single(chunks), whole, sems, ff_shard, t)
+        at = pl.ds(pl.multiple_of(t * SLICE, SLICE), SLICE)
     rows = rows_ref[...]
     gate = lax.dot_general(rows, whole[0, at], NT, preferred_element_type=F32)
     up = lax.dot_general(rows, whole[1, at], NT, preferred_element_type=F32)
@@ -1039,7 +1053,7 @@
 
     @pl.when(t == 0)
     def _():
-        acc[...] = more
+        acc[...] = before_ref[...] + more if last else more
 
     @pl.when(t > 0)
     def _():
@@ -1047,14 +1061,14 @@
 
     @pl.when(t == pl.num_programs(0) - 1)
     def _():
-        out_ref[...] = acc[...].astype(BF)
+        out_ref[...] = acc[...].astype(out_ref.dtype)
 
 
 def ffn_backward_kernel(count, ff_shard, grad_ref, act_ref, turn_ref, *refs):
     chunks, rest = refs[: count + 1], refs[count + 1 :]
     out_ref, dgate_ref, dup_ref, whole, acc, sems = rest
     t = pl.program_id(0)
-    fetch_weights(chunks, whole, sems, ff_shard, t)
+    fetch_weights(pair_last(chunks), whole, sems, ff_shard, t)
     at = pl.ds(pl.multiple_of(t * SLICE, SLICE), SLICE)
     dhid = lax.dot_general(grad_ref[...], whole[2, at], NT, preferred_element_type=F32)
     dgate = (dhid * turn_ref[0]).astype(BF)
@@ -1084,7 +1098,7 @@
     lead, first, ff_shard, rows_ref, grad_ref, hid_ref, dgate_ref, dup_ref, *refs
 ):
     chunks, (whole, sems) = refs[:-2], refs[-2:]
-    chunks = pair_first(chunks) if lead else [chunks[k : k + 1] for k in range(len(chunks))]
+    chunks = pair_last(chunks) if lead else single(chunks)
     base = first * ff_shard // SLICE
     t = pl.program_id(0)
     at = pl.ds(pl.multiple_of(t * SLICE, SLICE), SLICE)
@@ -1137,22 +1151,14 @@
     slots, count = rows.shape[0], len(chunks) - 1
     hidden = count * ff_shard
     steps = hidden // SLICE
-    return pl.pallas_call(
-        functools.partial(ffn_forward_kernel, count, ff_shard),
-        grid=(steps,),
-        out_shape=(
-            jax.ShapeDtypeStruct((slots, D), BF),
-            jax.ShapeDtypeStruct((steps, slots, SLICE), F32),
-            jax.ShapeDtypeStruct((steps, slots, SLICE), F32),
-            jax.ShapeDtypeStruct((steps, slots, SLICE), BF),
-        ),
-        in_specs=[fixed((slots, D))] + [ANY_SPEC] * (count + 1),
-        out_specs=(
-            fixed((slots, D)),
-            stepped((1, slots, SLICE)),
-            stepped((1, slots, SLICE)),
-            stepped((1, slots, SLICE)),
-        ),
+    near = (count - 1) * ff_shard // SLICE
+    tiles = [jax.ShapeDtypeStruct((steps, slots, SLICE), kind) for kind in (F32, F32, BF)]
+    part, *kept = pl.pallas_call(
+        functools.partial(ffn_forward_kernel, count, near, ff_shard, False),
+        grid=(near,),
+        out_shape=(jax.ShapeDtypeStruct((slots, D), F32), *tiles),
+        in_specs=[fixed((slots, D))] + [ANY_SPEC] * (count - 1),
+        out_specs=(fixed((slots, D)),) + (stepped((1, slots, SLICE)),) * 3,
         scratch_shapes=[
             pltpu.VMEM((3, hidden, D), BF),
             pltpu.VMEM((slots, D), F32),
@@ -1161,7 +1167,24 @@
         compiler_params=ffn_params(),
         cost_estimate=ffn_cost(slots, hidden),
         name="ffn_forward",
-    )(rows, *chunks)
+    )(rows, *chunks[: count - 1])
+    later = pl.BlockSpec((1, slots, SLICE), lambda t: (t + near, 0, 0))
+    return pl.pallas_call(
+        functools.partial(ffn_forward_kernel, count, near, ff_shard, True),
+        grid=(steps - near,),
+        out_shape=(jax.ShapeDtypeStruct((slots, D), BF), *tiles),
+        in_specs=[fixed((slots, D))] + [ANY_SPEC] * 3 + [fixed((slots, D))] + [ANY_SPEC] * 3,
+        out_specs=(fixed((slots, D)),) + (later,) * 3,
+        scratch_shapes=[
+            pltpu.VMEM((3, (steps - near + MARGIN) * SLICE, D), BF),
+            pltpu.VMEM((slots, D), F32),
+            pltpu.SemaphoreType.DMA((count, 4)),
+        ],
+        input_output_aliases={5: 1, 6: 2, 7: 3},
+        compiler_params=ffn_params(),
+        cost_estimate=ffn_cost(slots, ff_shard),
+        name="ffn_forward_last",
+    )(rows, *chunks[count - 2 :], part, *kept)
 
 
 def ffn_backward(grad, act, turn, chunks, ff_shard):
@@ -1188,13 +1211,17 @@
     )(grad, act, turn, *chunks)
 
 
+def count_hidden(tiles):
+    return tiles.shape[0] * SLICE
+
+
 def ffn_weights(rows, grad, hid, dgate, dup, first, last, ff_shard):
     slots = rows.shape[0]
-    lead = first == 0
+    lead = last * ff_shard == count_hidden(dgate)
     base, end = first * ff_shard // SLICE, -(-last * ff_shard // SLICE)
     full = jax.ShapeDtypeStruct((3 * ff_shard, D), BF)
     half = jax.ShapeDtypeStruct((3 * ff_shard // 2, D), BF)
-    shapes = ([half] * 2 if lead else [full]) + [full] * (last - first - 1)
+    shapes = [full] * (last - first - 1) + ([half] * 2 if lead else [full])
     tile = pl.BlockSpec((1, slots, SLICE), lambda t: (t + base, 0, 0))
     return pl.pallas_call(
         functools.partial(ffn_weights_kernel, lead, first, ff_shard),
@@ -1453,8 +1480,8 @@
     grad_result = swap_experts((slot_gate[:, None] * slot_grad).astype(BF))
 
     order = block_order(fsdp_count)
-    far = order[0]
-    blocks = list(weights.chunks[far]) + [weights.chunks[k] for k in order[1:]]
+    far = order[-1]
+    blocks = [weights.chunks[k] for k in order[:-1]] + list(weights.chunks[far])
     result_rows, act, turn, hidden = ffn_forward(expert_rows, blocks, ff_shard)
     returned = swap_experts(result_rows)
     grad_rows, grad_gate_pre, grad_up_pre = ffn_backward(
@@ -1462,10 +1489,11 @@
     )
     grad_sent = swap_experts(grad_rows)
     halves = (expert_rows, grad_result, hidden, grad_gate_pre, grad_up_pre)
-    early = ffn_weights(*halves, 0, 3, ff_shard)
-    late = ffn_weights(*halves, 3, fsdp_count, ff_shard)
-    totals = dict(zip(order[1:], early[2:] + late))
-    totals[far] = early[:2]
+    split = fsdp_count - 3
+    early = ffn_weights(*halves, split, fsdp_count, ff_shard)
+    late = ffn_weights(*halves, 0, split, ff_shard)
+    totals = dict(zip(order[:-1], late + early[:-2]))
+    totals[far] = early[-2:]
 
     def part(k):
         return totals[k]

time: 781 us -> 772 us (0.988)
  waiting for transfers between devices: 279 us -> 261 us
  Pallas kernels: 313 us -> 321 us
    ppermute x16, waiting for transfers between devices: 250 us -> 224 us  [ring_hop(): lax.ppermute(x, 'fsdp', [(ring[i], ring[(i + step) % count]) for i in ran...]
    pallas_call x1 -> x2, Pallas kernels: 34.7 us -> 42.5 us  [ffn_forward(): pl.pallas_call(functools.partial(ffn_forward_kernel, count, near, ff_shar...]
  transfers between devices with their start and end apart: 24 -> 24, of which waited for: 12 -> 9; matrix products, arithmetic and copies ran while one was open for 11% -> 11% of each run, Pallas kernels for 22% -> 24%
where the time goes in v2:
time: 772 us; the launch traced here: 763 us
  Pallas kernels  321 us (42%)
  waiting for transfers between devices  261 us (34%)
  starting transfers between devices  66.6 us (9%)
  local copies, waits for them, and re-layouts  49.5 us (6%)
  other arithmetic  35.6 us (5%)
  matrix products  24.6 us (3%)
    ppermute x16, waiting for transfers between devices, ring_hop(): lax.ppermute(x, 'fsdp', [(ring[i], ring[(i + step) % count]) for i in ran...  224 us
    pallas_call x1, Pallas kernels, dense_sum(): pl.pallas_call(functools.partial(dense_sum_kernel, cut), out_shape=jax.Sh...  69.6 us
    pallas_call x1, Pallas kernels, dense_gather(): pl.pallas_call(functools.partial(dense_gather_kernel, cut), out_shape=jax...  49.2 us
    pallas_call x1, Pallas kernels, attend_backward(): pl.pallas_call(functools.partial(attn_backward_kernel, sh), out_shape=(ja...  43.1 us
    pallas_call x2, Pallas kernels, ffn_forward(): pl.pallas_call(functools.partial(ffn_forward_kernel, count, near, ff_shar...  42.5 us
    pallas_call x1, Pallas kernels, ffn_backward(): pl.pallas_call(functools.partial(ffn_backward_kernel, count, ff_shard), g...  39.8 us
    pallas_call x2, Pallas kernels, ffn_weights(): pl.pallas_call(functools.partial(ffn_weights_kernel, lead, first, ff_shar...  31.6 us
    all_to_all x4, starting transfers between devices, swap_experts(): lax.all_to_all(rows, 'expert', split_axis=0, concat_axis=0, tiled=True)  27.1 us
  transfers between devices with their start and end apart: 24, of which 9 were waited for; matrix products, arithmetic and copies ran while one was open for 11% of the time, Pallas kernels for 24%

profile of v2, /device:TPU:11, one launch (start us, length us, event | category | flops | bytes accessed | tf_op | source)
XLA Modules:
  0.0 762.9 jit_solution(13249070417571017970)
XLA Ops:
  6.1 49.2 %dense_gather.1.wq_ref.wk_ref.wv_ref.w_ref = bf16[32,144,1024]{2,1,0:T(8,128)(2,1)} custom-call(bf16[144,1024]{1,0:T(8,128)(2,1)} %copy-done.34), custom_call_target="tpu_custom_call" | custom-call | bytes 100000000 | tf_op jit(solution)/shard_map/dense_gather/pallas_call | solution.py:764
  60.2 6.9 qkv_forward.1
  67.0 5.3 all-to-all-start
  74.3 97.1 %collective-permute-done.refs_2_ = bf16[1056,1024]{1,0:T(8,128)(2,1)} collective-permute-done((bf16[1056,1024]{1,0:T(8,128)(2,1)}, bf16[1056,1024]{1,0:T(8,128)(2,1)}, u32[]{:S(2)}, u32[]{:S(2)}) %collective-permute-start) | collective-permute-done | bytes 2162720 | tf_op jit(solution)/shard_map/ppermute | solution.py:526
  173.1 23.1 %attend_forward.1 = (bf16[8,384,128]{2,1,0:T(8,128)(2,1)}, f32[12,128,256]{2,1,0:T(8,128)S(1)}, f32[12,8,256]{2,1,0:T(8,128)S(1)}) custom-call(s32[8]{0:T(128)S(1)} %fusion.49.group_ref, f32[2,32]{1,0:T(2,128)S(1)} %fusion.51.table_ref, s32[9,128]{1,0:T(8,128)S(1)} %bitcast.87, bf16[8,384,384]{2,1,0:T(8,128)(2,1)S(1)} %all-to-all-done.x_ref), custom_call_target="tpu_custom_call" | custom-call | flops 10000000000 | bytes 8000000 | tf_op jit(solution)/shard_map/attend_forward/pallas_call | solution.py:465
  197.4 4.1 all-to-all-start.1
  202.2 3.2 slice.176
  207.8 11.3 %collective-permute-done.1.refs_4_ = bf16[1056,1024]{1,0:T(8,128)(2,1)} collective-permute-done((bf16[1056,1024]{1,0:T(8,128)(2,1)}, bf16[1056,1024]{1,0:T(8,128)(2,1)}, u32[]{:S(2)}, u32[]{:S(2)}) %collective-permute-start.1) | collective-permute-done | bytes 2162720 | tf_op jit(solution)/shard_map/ppermute | solution.py:526
  221.5 14.3 %all-to-all-done.1 = bf16[8,384,128]{2,1,0:T(8,128)(2,1)S(1)} async-done(((bf16[8,384,128]{2,1,0:T(8,128)(2,1)}), bf16[8,384,128]{2,1,0:T(8,128)(2,1)S(1)}, u32[]{:S(2)}, u32[]{:S(2)}) %all-to-all-start.1) | async-done | bytes 786464 | tf_op jit(solution)/shard_map/all_to_all | solution.py:1447
  236.1 3.0 multiply_reduce_fusion.2
  239.1 2.6 convolution_convert_fusion.1
  241.8 9.1 %all-to-all-start.2 = ((bf16[4,240,1024]{2,1,0:T(8,128)(2,1)}), bf16[4,240,1024]{2,1,0:T(8,128)(2,1)}, u32[]{:S(2)}, u32[]{:S(2)}) async-start(bf16[4,240,1024]{2,1,0:T(8,128)(2,1)} %bitcast.107), calls=%async_computation.2 | async-start | bytes 3932160 | tf_op jit(solution)/shard_map/all_to_all | solution.py:1471
  253.2 2.5 multiply_convert_fusion
  255.7 26.3 %collective-permute-done.5.refs_5_ = bf16[1056,1024]{1,0:T(8,128)(2,1)} collective-permute-done((bf16[1056,1024]{1,0:T(8,128)(2,1)}, bf16[1056,1024]{1,0:T(8,128)(2,1)}, u32[]{:S(2)}, u32[]{:S(2)}) %collective-permute-start.5) | collective-permute-done | bytes 2162720 | tf_op jit(solution)/shard_map/ppermute | solution.py:526
  281.9 2.3 slice.226
  286.4 2.3 slice.227
  288.7 7.7 %all-to-all-start.4 = ((bf16[4,240,1024]{2,1,0:T(8,128)(2,1)}), bf16[4,240,1024]{2,1,0:T(8,128)(2,1)}, u32[]{:S(2)}, u32[]{:S(2)}) async-start(bf16[4,240,1024]{2,1,0:T(8,128)(2,1)} %bitcast.108), calls=%async_computation.4 | async-start | bytes 3932160 | tf_op jit(solution)/shard_map/all_to_all | solution.py:1471
  296.4 29.9 %ffn_forward.1 = (f32[960,1024]{1,0:T(8,128)}, f32[11,960,256]{2,1,0:T(8,128)}, f32[11,960,256]{2,1,0:T(8,128)}, bf16[11,960,256]{2,1,0:T(8,128)(2,1)}) custom-call(bf16[960,1024]{1,0:T(8,128)(2,1)} %bitcast.18.rows_ref, bf16[1056,1024]{1,0:T(8,128)(2,1)} %pad_maximum_fusion.refs_0_, bf16[1056,1024]{1,0:T(8,128)(2,1)} %collective-permute-done.3.refs_1_, ...), custom_call_target="tpu_custom_call" | custom-call | flops 16609443840 | bytes 40000000 | tf_op jit(solution)/shard_map/ffn_forward/pallas_call | solution.py:1156
  327.3 12.6 %ffn_forward_last.1 = (bf16[960,1024]{1,0:T(8,128)(2,1)}, f32[11,960,256]{2,1,0:T(8,128)}, f32[11,960,256]{2,1,0:T(8,128)}, bf16[11,960,256]{2,1,0:T(8,128)(2,1)}) custom-call(bf16[960,1024]{1,0:T(8,128)(2,1)} %bitcast.18.rows_ref, ...), custom_call_target="tpu_custom_call", output_to_operand_aliasing={{1}: (5, {}), {2}: (6, {}), {3}: (7, {})} | custom-call | flops 2076180480 | bytes 40000000 | tf_op jit(solution)/shard_map/ffn_forward_last/pallas_call | solution.py:1172
  340.0 4.7 all-to-all-start.3
  344.7 39.8 %ffn_backward.1 = (bf16[960,1024]{1,0:T(8,128)(2,1)}, bf16[11,960,256]{2,1,0:T(8,128)(2,1)}, bf16[11,960,256]{2,1,0:T(8,128)(2,1)}) custom-call(bf16[960,1024]{1,0:T(8,128)(2,1)} %bitcast.31.grad_ref, f32[11,960,256]{2,1,0:T(8,128)} %get-tuple-element.59.act_ref, f32[11,960,256]{2,1,0:T(8,128)} %get-tuple-element.60.turn_ref, ...), custom_call_target="tpu_custom_call" | custom-call | flops 16609443840 | bytes 40000000 | tf_op jit(solution)/shard_map/ffn_backward/pallas_call | solution.py:1195
  384.5 13.7 %shard_map.247 = (bf16[1056,1024]{1,0:T(8,128)(2,1)}, bf16[1056,1024]{1,0:T(8,128)(2,1)}, bf16[528,1024]{1,0:T(8,128)(2,1)}, bf16[528,1024]{1,0:T(8,128)(2,1)}) custom-call(bf16[960,1024]{1,0:T(8,128)(2,1)} %bitcast.18.rows_ref, bf16[960,1024]{1,0:T(8,128)(2,1)} %bitcast.31.grad_ref, bf16[11,960,256]{2,1,0:T(8,128)(2,1)} %get-tuple-element.62.hid_ref, ...), custom_call_target="tpu_custom_call" | custom-call | flops 7549747200 | bytes 40000000 | tf_op jit(solution)/shard_map/pallas_call | solution.py:1226
  400.7 2.4 slice.195
  404.1 19.5 %collective-permute-done.8 = bf16[528,1024]{1,0:T(8,128)(2,1)S(1)} collective-permute-done((bf16[528,1024]{1,0:T(8,128)(2,1)}, bf16[528,1024]{1,0:T(8,128)(2,1)S(1)}, u32[]{:S(2)}, u32[]{:S(2)}) %collective-permute-start.8) | collective-permute-done | bytes 1081376 | tf_op jit(solution)/shard_map/ppermute | solution.py:526
  424.1 5.5 all-to-all-start.5
  429.6 2.9 pad_maximum_fusion.1
  437.8 2.6 fusion.6
  440.5 3.8 fusion.4
  444.2 7.9 %all-to-all-done.5 = bf16[4,240,1024]{2,1,0:T(8,128)(2,1)} async-done(((bf16[4,240,1024]{2,1,0:T(8,128)(2,1)}), bf16[4,240,1024]{2,1,0:T(8,128)(2,1)}, u32[]{:S(2)}, u32[]{:S(2)}) %all-to-all-start.5) | async-done | bytes 1966112 | tf_op jit(solution)/shard_map/all_to_all | solution.py:1471
  452.1 2.6 fusion.16
  461.0 4.6 all-to-all-start.6
  465.6 17.9 %shard_map.248 = (bf16[1056,1024]{1,0:T(8,128)(2,1)}, bf16[1056,1024]{1,0:T(8,128)(2,1)}, bf16[1056,1024]{1,0:T(8,128)(2,1)}, bf16[1056,1024]{1,0:T(8,128)(2,1)}, bf16[1056,1024]{1,0:T(8,128)(2,1)}) custom-call(bf16[960,1024]{1,0:T(8,128)(2,1)} %bitcast.18.rows_ref, bf16[960,1024]{1,0:T(8,128)(2,1)} %bitcast.31.grad_ref, ...), custom_call_target="tpu_custom_call" | custom-call | flops 10569646080 | bytes 40000000 | tf_op jit(solution)/shard_map/pallas_call | solution.py:1226
  483.5 15.0 %all-to-all-done.6.do_ref = bf16[8,384,128]{2,1,0:T(8,128)(2,1)S(1)} async-done(((bf16[8,384,128]{2,1,0:T(8,128)(2,1)}), bf16[8,384,128]{2,1,0:T(8,128)(2,1)S(1)}, u32[]{:S(2)}, u32[]{:S(2)}) %all-to-all-start.6) | async-done | bytes 786464 | tf_op jit(solution)/shard_map/all_to_all | solution.py:1524
  498.5 3.4 add_convert_fusion.3
  501.9 3.8 collective-permute-start.12
  505.6 2.7 add_convert_fusion.2
  510.4 43.1 %attend_backward.1 = (bf16[8,384,384]{2,1,0:T(8,128)(2,1)S(1)}, f32[64,128]{1,0:T(8,128)S(1)}) custom-call(s32[8]{0:T(128)S(1)} %fusion.49.group_ref, f32[2,32]{1,0:T(2,128)S(1)} %fusion.51.table_ref, s32[9,128]{1,0:T(8,128)S(1)} %bitcast.88, bf16[8,384,384]{2,1,0:T(8,128)(2,1)} %copy-done.2, bf16[8,384,128]{2,1,0:T(8,128)(2,1)S(1)} %all-to-all-done.6.do_ref, ...), custom_call_target="tpu_custom_call" | custom-call | flops 20000000000 | bytes 12000000 | tf_op jit(solution)/shard_map/attend_backward/pallas_call | solution.py:490
  555.0 6.6 all-to-all-start.7
  561.6 4.8 add_convert_fusion
  566.5 4.0 add_convert_fusion.1
  575.6 2.6 convolution_convert_fusion
  578.3 6.6 pad.13.kept_ref
  588.9 69.3 %collective-permute-done.15 = bf16[1056,1024]{1,0:T(8,128)(2,1)} collective-permute-done((bf16[1056,1024]{1,0:T(8,128)(2,1)}, bf16[1056,1024]{1,0:T(8,128)(2,1)}, u32[]{:S(2)}, u32[]{:S(2)}) %collective-permute-start.15) | collective-permute-done | bytes 2162720 | tf_op jit(solution)/shard_map/ppermute | solution.py:526
  659.1 4.4 convert_add_fusion
  663.5 2.2 slice_bitcast_fusion
  665.7 15.6 %qkv_backward.1 = (bf16[32,144,1024]{2,1,0:T(8,128)(2,1)}, f32[384,1024]{1,0:T(8,128)S(1)}, f32[8,1024]{1,0:T(8,128)S(1)}) custom-call(bf16[8,384,384]{2,1,0:T(8,128)(2,1)} %all-to-all-done.7.dq_ref, bf16[384,1024]{1,0:T(8,128)(2,1)S(1)} %copy-done.4, bf16[32,144,1024]{2,1,0:T(8,128)(2,1)} %dense_gather.1.wq_ref.wk_ref.wv_ref.w_ref, ...), custom_call_target="tpu_custom_call", output_to_operand_aliasing={{0}: (6, {})} | custom-call | flops 4831838208 | bytes 25000000 | tf_op jit(solution)/shard_map/qkv_backward/pallas_call | solution.py:1323
  683.2 3.7 copy-done
  686.9 69.6 %dense_sum.1 = f32[144,1024]{1,0:T(8,128)S(1)} custom-call(bf16[32,144,1024]{2,1,0:T(8,128)(2,1)S(1)} %copy-done), custom_call_target="tpu_custom_call" | custom-call | bytes 100000000 | tf_op jit(solution)/shard_map/dense_sum/pallas_call | solution.py:928
  (251 shorter events, 61.3 us)
Async XLA Ops:
  1.7 57.4 %copy-start.17 = (bf16[128,1024]{1,0:T(8,128)(2,1)}, bf16[128,1024]{1,0:T(8,128)(2,1)S(1)}, u32[]{:S(2)}) copy-start(bf16[128,1024]{1,0:T(8,128)(2,1)S(1)} %slice.168) | copy-start | bytes 786436
  6.1 50.4 %copy-start.31 = (bf16[1,352,1024]{2,1,0:T(8,128)(2,1)S(1)}, bf16[1,352,1024]{2,1,0:T(8,128)(2,1)}, u32[]{:S(2)}) copy-start(bf16[1,352,1024]{2,1,0:T(8,128)(2,1)} %param.25) | copy-start | bytes 2162692
  6.1 50.4 %copy-start.32 = (bf16[1,1024,352]{1,2,0:T(8,128)(2,1)S(1)}, bf16[1,1024,352]{1,2,0:T(8,128)(2,1)}, u32[]{:S(2)}) copy-start(bf16[1,1024,352]{1,2,0:T(8,128)(2,1)} %param.24) | copy-start | bytes 2162692
  6.1 50.4 %copy-start.33 = (bf16[1,1024,352]{1,2,0:T(8,128)(2,1)S(1)}, bf16[1,1024,352]{1,2,0:T(8,128)(2,1)}, u32[]{:S(2)}) copy-start(bf16[1,1024,352]{1,2,0:T(8,128)(2,1)} %param.23) | copy-start | bytes 2162692
  58.4 8.7 %copy-start.14 = (bf16[128,2,1024]{2,0,1:T(8,128)(2,1)}, bf16[128,2,1024]{2,0,1:T(8,128)(2,1)S(1)}, u32[]{:S(2)}) copy-start(bf16[128,2,1024]{2,0,1:T(8,128)(2,1)S(1)} %copy.52) | copy-start | bytes 1572868
  67.0 106.1 %copy-start.6 = (s32[1152]{0:T(1024)S(1)}, s32[1152]{0:T(1024)}, u32[]{:S(2)}) copy-start(s32[1152]{0:T(1024)} %param.29) | copy-start | bytes 13828
  67.0 106.1 %all-to-all-start = ((bf16[8,384,384]{2,1,0:T(8,128)(2,1)}), bf16[8,384,384]{2,1,0:T(8,128)(2,1)S(1)}, u32[]{:S(2)}, u32[]{:S(2)}) async-start(bf16[8,384,384]{2,1,0:T(8,128)(2,1)} %get-tuple-element.51), calls=%async_computation | async-start | bytes 4718592 | tf_op jit(solution)/shard_map/all_to_all | solution.py:1444
  72.4 99.0 %collective-permute-start = (bf16[1056,1024]{1,0:T(8,128)(2,1)}, bf16[1056,1024]{1,0:T(8,128)(2,1)}, u32[]{:S(2)}, u32[]{:S(2)}) collective-permute-start(bf16[1056,1024]{1,0:T(8,128)(2,1)} %pad_maximum_fusion.refs_0_), channel_id=1, source_target_pairs={{0,1},{2,0},{4,2},{6,4},{7,6},{5,7},{3,5},{1,3},{8,9},{10,8},{12,1... | collective-permute-start | bytes 6488072 | tf_op jit(solution)/shard_map/ppermute | solution.py:526
  72.4 99.0 %collective-permute-start.3 = (bf16[1056,1024]{1,0:T(8,128)(2,1)}, bf16[1056,1024]{1,0:T(8,128)(2,1)}, u32[]{:S(2)}, u32[]{:S(2)}) collective-permute-start(bf16[1056,1024]{1,0:T(8,128)(2,1)} %pad_maximum_fusion.refs_0_), channel_id=1, source_target_pairs={{0,2},{2,4},{4,6},{6,7},{7,5},{5,3},{3,1},{1,0},{8,10},{10,12},{12... | collective-permute-start | bytes 6488072 | tf_op jit(solution)/shard_map/ppermute | solution.py:526
  171.3 47.8 %collective-permute-start.1 = (bf16[1056,1024]{1,0:T(8,128)(2,1)}, bf16[1056,1024]{1,0:T(8,128)(2,1)}, u32[]{:S(2)}, u32[]{:S(2)}) collective-permute-start(bf16[1056,1024]{1,0:T(8,128)(2,1)} %collective-permute-done.refs_2_), channel_id=1, source_target_pairs={{0,1},{2,0},{4,2},{6,4},{7,6},{5,7},{3,5},{1,3},{8,9},{10,8},{12,1... | collective-permute-start | bytes 6488072 | tf_op jit(solution)/shard_map/ppermute | solution.py:526
  171.4 48.1 %collective-permute-start.4 = (bf16[1056,1024]{1,0:T(8,128)(2,1)}, bf16[1056,1024]{1,0:T(8,128)(2,1)}, u32[]{:S(2)}, u32[]{:S(2)}) collective-permute-start(bf16[1056,1024]{1,0:T(8,128)(2,1)} %collective-permute-done.3.refs_1_), channel_id=1, source_target_pairs={{0,2},{2,4},{4,6},{6,7},{7,5},{5,3},{3,1},{1,0},{8,10},{10,12},{12... | collective-permute-start | bytes 6488072 | tf_op jit(solution)/shard_map/ppermute | solution.py:526
  173.1 23.1 %copy-start.2 = (bf16[8,384,384]{2,1,0:T(8,128)(2,1)}, bf16[8,384,384]{2,1,0:T(8,128)(2,1)S(1)}, u32[]{:S(2)}) copy-start(bf16[8,384,384]{2,1,0:T(8,128)(2,1)S(1)} %all-to-all-done.x_ref) | copy-start | bytes 7077892
  173.1 28.3 %copy-start.23 = (bf16[384,1024]{1,0:T(8,128)(2,1)S(1)}, bf16[384,1024]{1,0:T(8,128)(2,1)}, u32[]{:S(2)}) copy-start(bf16[384,1024]{1,0:T(8,128)(2,1)} %param.30) | copy-start | bytes 2359300
  197.4 38.4 %all-to-all-start.1 = ((bf16[8,384,128]{2,1,0:T(8,128)(2,1)}), bf16[8,384,128]{2,1,0:T(8,128)(2,1)S(1)}, u32[]{:S(2)}, u32[]{:S(2)}) async-start(bf16[8,384,128]{2,1,0:T(8,128)(2,1)} %get-tuple-element.52), calls=%async_computation.1 | async-start | bytes 1572864 | tf_op jit(solution)/shard_map/all_to_all | solution.py:1447
  205.7 30.4 %copy-start.15 = (bf16[128,2,1024]{2,0,1:T(8,128)(2,1)S(1)}, bf16[128,2,1024]{2,0,1:T(8,128)(2,1)}, u32[]{:S(2)}) copy-start(bf16[128,2,1024]{2,0,1:T(8,128)(2,1)} %copy-done.14) | copy-start | bytes 1572868
  206.7 250.1 %copy-start.37 = (f32[1024]{0:T(1024)}, f32[1024]{0:T(1024)S(1)}, u32[]{:S(2)}) copy-start(f32[1024]{0:T(1024)S(1)} %reshape.270) | copy-start | bytes 12292
  219.1 67.3 %collective-permute-start.2 = (bf16[1056,1024]{1,0:T(8,128)(2,1)}, bf16[1056,1024]{1,0:T(8,128)(2,1)}, u32[]{:S(2)}, u32[]{:S(2)}) collective-permute-start(bf16[1056,1024]{1,0:T(8,128)(2,1)} %collective-permute-done.1.refs_4_), channel_id=1, source_target_pairs={{0,1},{2,0},{4,2},{6,4},{7,6},{5,7},{3,5},{1,3},{8,9},{10,8},{12,1... | collective-permute-start | bytes 6488072 | tf_op jit(solution)/shard_map/ppermute | solution.py:526
  219.4 62.5 %collective-permute-start.5 = (bf16[1056,1024]{1,0:T(8,128)(2,1)}, bf16[1056,1024]{1,0:T(8,128)(2,1)}, u32[]{:S(2)}, u32[]{:S(2)}) collective-permute-start(bf16[1056,1024]{1,0:T(8,128)(2,1)} %collective-permute-done.4.refs_3_), channel_id=1, source_target_pairs={{0,2},{2,4},{4,6},{6,7},{7,5},{5,3},{3,1},{1,0},{8,10},{10,12},{12... | collective-permute-start | bytes 6488072 | tf_op jit(solution)/shard_map/ppermute | solution.py:526
  239.1 217.7 %copy-start.9 = (f32[384,1024]{1,0:T(8,128)}, f32[384,1024]{1,0:T(8,128)S(1)}, u32[]{:S(2)}) copy-start(f32[384,1024]{1,0:T(8,128)S(1)} %get-tuple-element.163) | copy-start | bytes 4718596
  239.1 217.7 %copy-start.42 = (f32[384]{0:T(512)}, f32[384]{0:T(512)S(1)}, u32[]{:S(2)}) copy-start(f32[384]{0:T(512)S(1)} %fusion.43) | copy-start | bytes 4612
  241.8 11.4 %copy-start.24 = (bf16[128,2,1024]{2,0,1:T(8,128)(2,1)S(1)}, bf16[128,2,1024]{2,0,1:T(8,128)(2,1)}, u32[]{:S(2)}) copy-start(bf16[128,2,1024]{2,0,1:T(8,128)(2,1)} %copy.58) | copy-start | bytes 1572868
  241.8 11.4 %copy-start.28 = (bf16[128,1024]{1,0:T(8,128)(2,1)S(1)}, bf16[128,1024]{1,0:T(8,128)(2,1)}, u32[]{:S(2)}) copy-start(bf16[128,1024]{1,0:T(8,128)(2,1)} %slice.194) | copy-start | bytes 786436
  241.8 47.0 %all-to-all-start.2 = ((bf16[4,240,1024]{2,1,0:T(8,128)(2,1)}), bf16[4,240,1024]{2,1,0:T(8,128)(2,1)}, u32[]{:S(2)}, u32[]{:S(2)}) async-start(bf16[4,240,1024]{2,1,0:T(8,128)(2,1)} %bitcast.107), calls=%async_computation.2 | async-start | bytes 3932160 | tf_op jit(solution)/shard_map/all_to_all | solution.py:1471
  251.9 203.0 %copy-start.35 = (f32[384,4]{0,1:T(4,128)}, f32[384,4]{0,1:T(4,128)S(1)}, u32[]{:S(2)}) copy-start(f32[384,4]{0,1:T(4,128)S(1)} %get-tuple-element.165) | copy-start | bytes 18436
  251.9 203.0 %copy-start.44 = (f32[384]{0:T(512)}, f32[384]{0:T(512)S(1)}, u32[]{:S(2)}) copy-start(f32[384]{0:T(512)S(1)} %is-finite_select_fusion) | copy-start | bytes 4612
  284.2 42.1 %collective-permute-start.6 = (bf16[528,1024]{1,0:T(8,128)(2,1)}, bf16[528,1024]{1,0:T(8,128)(2,1)S(1)}, u32[]{:S(2)}, u32[]{:S(2)}) collective-permute-start(bf16[528,1024]{1,0:T(8,128)(2,1)} %slice.226), channel_id=1, source_target_pairs={{0,2},{2,4},{4,6},{6,7},{7,5},{5,3},{3,1},{1,0},{8,10},{10,12},{12... | collective-permute-start | bytes 3244040 | tf_op jit(solution)/shard_map/ppermute | solution.py:526
  288.7 37.7 %collective-permute-start.7 = (bf16[528,1024]{1,0:T(8,128)(2,1)}, bf16[528,1024]{1,0:T(8,128)(2,1)}, u32[]{:S(2)}, u32[]{:S(2)}) collective-permute-start(bf16[528,1024]{1,0:T(8,128)(2,1)} %slice.227), channel_id=1, source_target_pairs={{0,1},{2,0},{4,2},{6,4},{7,6},{5,7},{3,5},{1,3},{8,9},{10,8},{12,1... | collective-permute-start | bytes 3244040 | tf_op jit(solution)/shard_map/ppermute | solution.py:526
  288.7 51.2 %all-to-all-start.4 = ((bf16[4,240,1024]{2,1,0:T(8,128)(2,1)}), bf16[4,240,1024]{2,1,0:T(8,128)(2,1)}, u32[]{:S(2)}, u32[]{:S(2)}) async-start(bf16[4,240,1024]{2,1,0:T(8,128)(2,1)} %bitcast.108), calls=%async_computation.4 | async-start | bytes 3932160 | tf_op jit(solution)/shard_map/all_to_all | solution.py:1471
  340.0 84.1 %all-to-all-start.3 = ((bf16[4,240,1024]{2,1,0:T(8,128)(2,1)}), bf16[4,240,1024]{2,1,0:T(8,128)(2,1)}, u32[]{:S(2)}, u32[]{:S(2)}) async-start(bf16[4,240,1024]{2,1,0:T(8,128)(2,1)} %bitcast.106), calls=%async_computation.3 | async-start | bytes 3932160 | tf_op jit(solution)/shard_map/all_to_all | solution.py:1471
  398.2 25.4 %collective-permute-start.8 = (bf16[528,1024]{1,0:T(8,128)(2,1)}, bf16[528,1024]{1,0:T(8,128)(2,1)S(1)}, u32[]{:S(2)}, u32[]{:S(2)}) collective-permute-start(bf16[528,1024]{1,0:T(8,128)(2,1)} %get-tuple-element.66), channel_id=1, source_target_pairs={{0,2},{2,4},{4,6},{6,7},{7,5},{5,3},{3,1},{1,0},{8,10},{10,12},{12... | collective-permute-start | bytes 3244040 | tf_op jit(solution)/shard_map/ppermute | solution.py:526
  400.0 34.3 %collective-permute-start.10 = (bf16[528,1024]{1,0:T(8,128)(2,1)}, bf16[528,1024]{1,0:T(8,128)(2,1)}, u32[]{:S(2)}, u32[]{:S(2)}) collective-permute-start(bf16[528,1024]{1,0:T(8,128)(2,1)} %get-tuple-element.68), channel_id=1, source_target_pairs={{0,1},{2,0},{4,2},{6,4},{7,6},{5,7},{3,5},{1,3},{8,9},{10,8},{12,1... | collective-permute-start | bytes 3244040 | tf_op jit(solution)/shard_map/ppermute | solution.py:526
  400.7 23.0 %copy-start.22 = (bf16[1056,1024]{1,0:T(8,128)(2,1)S(1)}, bf16[1056,1024]{1,0:T(8,128)(2,1)}, u32[]{:S(2)}) copy-start(bf16[1056,1024]{1,0:T(8,128)(2,1)} %get-tuple-element.65) | copy-start | bytes 6488068
  424.1 28.1 %all-to-all-start.5 = ((bf16[4,240,1024]{2,1,0:T(8,128)(2,1)}), bf16[4,240,1024]{2,1,0:T(8,128)(2,1)}, u32[]{:S(2)}, u32[]{:S(2)}) async-start(bf16[4,240,1024]{2,1,0:T(8,128)(2,1)} %bitcast.105), calls=%async_computation.5 | async-start | bytes 3932160 | tf_op jit(solution)/shard_map/all_to_all | solution.py:1471
  432.6 65.9 %collective-permute-start.9 = (bf16[1056,1024]{1,0:T(8,128)(2,1)}, bf16[1056,1024]{1,0:T(8,128)(2,1)}, u32[]{:S(2)}, u32[]{:S(2)}) collective-permute-start(bf16[1056,1024]{1,0:T(8,128)(2,1)} %pad_maximum_fusion.1), channel_id=1, source_target_pairs={{0,2},{2,4},{4,6},{6,7},{7,5},{5,3},{3,1},{1,0},{8,10},{10,12},{12... | collective-permute-start | bytes 6488072 | tf_op jit(solution)/shard_map/ppermute | solution.py:526
  437.6 60.9 %collective-permute-start.11 = (bf16[1056,1024]{1,0:T(8,128)(2,1)}, bf16[1056,1024]{1,0:T(8,128)(2,1)}, u32[]{:S(2)}, u32[]{:S(2)}) collective-permute-start(bf16[1056,1024]{1,0:T(8,128)(2,1)} %pad_maximum_fusion.2), channel_id=1, source_target_pairs={{0,1},{2,0},{4,2},{6,4},{7,6},{5,7},{3,5},{1,3},{8,9},{10,8},{12,1... | collective-permute-start | bytes 6488072 | tf_op jit(solution)/shard_map/ppermute | solution.py:526
  461.0 37.4 %all-to-all-start.6 = ((bf16[8,384,128]{2,1,0:T(8,128)(2,1)}), bf16[8,384,128]{2,1,0:T(8,128)(2,1)S(1)}, u32[]{:S(2)}, u32[]{:S(2)}) async-start(bf16[8,384,128]{2,1,0:T(8,128)(2,1)} %bitcast.35), calls=%async_computation.6 | async-start | bytes 1572864 | tf_op jit(solution)/shard_map/all_to_all | solution.py:1524
  498.4 7.2 copy-start.19
  501.9 53.1 %collective-permute-start.12 = (bf16[1056,1024]{1,0:T(8,128)(2,1)S(1)}, bf16[1056,1024]{1,0:T(8,128)(2,1)}, u32[]{:S(2)}, u32[]{:S(2)}) collective-permute-start(bf16[1056,1024]{1,0:T(8,128)(2,1)S(1)} %add_convert_fusion.3), channel_id=1, source_target_pairs={{0,2},{2,4},{4,6},{6,7},{7,5},{5,3},{3,1},{1,0},{8,10},{10,12},{12... | collective-permute-start | bytes 6488072 | tf_op jit(solution)/shard_map/ppermute | solution.py:526
  508.4 46.6 %collective-permute-start.13 = (bf16[1056,1024]{1,0:T(8,128)(2,1)S(1)}, bf16[1056,1024]{1,0:T(8,128)(2,1)}, u32[]{:S(2)}, u32[]{:S(2)}) collective-permute-start(bf16[1056,1024]{1,0:T(8,128)(2,1)S(1)} %add_convert_fusion.2), channel_id=1, source_target_pairs={{0,1},{2,0},{4,2},{6,4},{7,6},{5,7},{3,5},{1,3},{8,9},{10,8},{12,1... | collective-permute-start | bytes 6488072 | tf_op jit(solution)/shard_map/ppermute | solution.py:526
  555.0 110.7 %all-to-all-start.7 = ((bf16[8,384,384]{2,1,0:T(8,128)(2,1)}), bf16[8,384,384]{2,1,0:T(8,128)(2,1)}, u32[]{:S(2)}, u32[]{:S(2)}) async-start(bf16[8,384,384]{2,1,0:T(8,128)(2,1)} %copy-done.3), calls=%async_computation.7 | async-start | bytes 4718592 | tf_op jit(solution)/shard_map/all_to_all | solution.py:1532
  566.3 91.9 %collective-permute-start.15 = (bf16[1056,1024]{1,0:T(8,128)(2,1)}, bf16[1056,1024]{1,0:T(8,128)(2,1)}, u32[]{:S(2)}, u32[]{:S(2)}) collective-permute-start(bf16[1056,1024]{1,0:T(8,128)(2,1)} %add_convert_fusion), channel_id=1, source_target_pairs={{0,1},{2,0},{4,2},{6,4},{7,6},{5,7},{3,5},{1,3},{8,9},{10,8},{12,1... | collective-permute-start | bytes 6488072 | tf_op jit(solution)/shard_map/ppermute | solution.py:526
  566.5 7.5 copy-start.30
  570.5 88.6 %collective-permute-start.14 = (bf16[1056,1024]{1,0:T(8,128)(2,1)}, bf16[1056,1024]{1,0:T(8,128)(2,1)}, u32[]{:S(2)}, u32[]{:S(2)}) collective-permute-start(bf16[1056,1024]{1,0:T(8,128)(2,1)} %add_convert_fusion.1), channel_id=1, source_target_pairs={{0,2},{2,4},{4,6},{6,7},{7,5},{5,3},{3,1},{1,0},{8,10},{10,12},{12... | collective-permute-start | bytes 6488072 | tf_op jit(solution)/shard_map/ppermute | solution.py:526
  578.3 6.6 copy-start.38
  578.3 6.6 copy-start.41
  578.3 6.6 copy-start.43
  578.3 6.6 copy-start.45
  578.3 6.6 copy-start.47
  (35 other events, 108.5 us)
